TPU v7x, 512 devices: a whole 4x4x16 slice. The times are simulated.
512 devices in a mesh: seq: 128 (over z, y, core), fsdp: 4 (over x).
Axes of the slice: x: 4, y: 4, z: 16, core: 2. Of those that a mesh axis runs over, the one named last changes fastest.
Arguments:
- tokens: bfloat16 [4, 65536, 2048], P('fsdp', 'seq'), may hold values from -9 to 9
- qkv_weight: bfloat16 [2048, 1536], P('fsdp'), may hold values from -0.26516504 to 0.26516504
- near_offset: int32 [4], replicated, may hold values from 0 to 3
- far_offset: int32 [4], replicated, may hold values from 0 to 31
Outputs:
- mixed: bfloat16 [4, 65536, 512], P('fsdp', 'seq')
All inputs are finite; a program needn't handle non-finite values.
Results may differ from a plain program's by a relative error of at most 0.0074.
Values may be sent and summed in bfloat16 or wider, within the bound.
A program may use at most 64 MiB of HBM per device.

v0:
```python
import jax
import jax.numpy as jnp
from jax import lax
from jax.sharding import PartitionSpec as P

HEADS = 4
HEAD_DIM = 128
BLOCK = 128
STRIDE = 8


NEG = -1e30


def from_behind(value, axis, steps):
    count = lax.axis_size(axis)
    first, last = (max(0, -steps), min(count, count - steps))
    return lax.ppermute(value, axis, [(source, source + steps) for source in range(first, last)])


def level_stats(query, key_rows, value_rows, distance):
    scores = jnp.einsum(
        "hqd,hkd->hqk", query, key_rows, preferred_element_type=jnp.float32
    ) * HEAD_DIM ** (-0.5)
    key_count = key_rows.shape[1]
    key_place = jnp.arange(key_count) % BLOCK
    key_distance = jnp.repeat(distance, BLOCK)
    query_place = jnp.arange(BLOCK)
    visible = (key_distance[None, :] > 0) | (key_distance[None, :] == 0) & (
        key_place[None, :] <= query_place[:, None]
    )
    scores = jnp.where(visible[None], scores, NEG)
    best_score = jnp.max(scores, axis=2)
    weights = jnp.exp(scores - best_score[..., None])
    weight_sum = jnp.sum(weights, axis=2)
    weighted = jnp.einsum(
        "hqk,hkd->hqd", weights.astype(jnp.bfloat16), value_rows, preferred_element_type=jnp.float32
    )
    return (best_score, weight_sum, weighted)


def near_shifts(key_value, group_size, position):
    key_list = []
    value_list = []
    distance_list = []
    for shift_by in range(group_size - 1, 0, -1):
        arrived = from_behind((key_value[0], key_value[1]), "seq", shift_by)
        key_list.append(arrived[0])
        value_list.append(arrived[1])
        distance_list.append(jnp.where(position >= shift_by, shift_by, -1).astype(jnp.int32))
    key_list.append(key_value[0])
    value_list.append(key_value[1])
    distance_list.append(jnp.zeros((), jnp.int32))
    return (
        jnp.concatenate(key_list, axis=1),
        jnp.concatenate(value_list, axis=1),
        jnp.stack(distance_list),
    )


def far_shifts(key_value, group_size, position):
    key_list = []
    value_list = []
    distance_list = []
    for shift_by in range(group_size - 1, 0, -1):
        arrived = from_behind((key_value[0], key_value[1]), "seq", shift_by * STRIDE)
        key_list.append(arrived[0])
        value_list.append(arrived[1])
        distance_list.append(jnp.where(position >= shift_by, shift_by, -1).astype(jnp.int32))
    key_list.append(key_value[0])
    value_list.append(key_value[1])
    distance_list.append(jnp.zeros((), jnp.int32))
    return (
        jnp.concatenate(key_list, axis=1),
        jnp.concatenate(value_list, axis=1),
        jnp.stack(distance_list),
    )


def body(tokens, qkv_weight, near_offset, far_offset):
    sequence = tokens[0]
    row_count = sequence.shape[0]
    qkv_width = HEADS * HEAD_DIM
    block_rate = row_count // BLOCK
    seq_size = lax.axis_size("seq")
    seq_index = lax.axis_index("seq")
    near_size = min(16, seq_size)
    half_size = near_size // 2
    far_size = min(16, seq_size // STRIDE)
    projected = jnp.dot(
        sequence,
        lax.all_gather(qkv_weight, "fsdp", axis=0, tiled=True),
        preferred_element_type=jnp.float32,
    ).astype(jnp.bfloat16)
    query = projected[:, :qkv_width].reshape(row_count, HEADS, HEAD_DIM)
    key_all = projected[:, qkv_width : 2 * qkv_width].reshape(row_count, HEADS, HEAD_DIM)
    value_all = projected[:, 2 * qkv_width :].reshape(row_count, HEADS, HEAD_DIM)
    local_scores = jnp.einsum(
        "qhd,khd->hqk", query, key_all, preferred_element_type=jnp.float32
    ) * HEAD_DIM ** (-0.5)
    positions = jnp.arange(row_count)
    local_scores = jnp.where((positions[None, :] <= positions[:, None])[None], local_scores, NEG)
    local_top = jnp.max(local_scores, axis=2)
    local_probs = jnp.exp(local_scores - local_top[..., None])
    local_sum = jnp.sum(local_probs, axis=2)
    local_out = jnp.einsum(
        "hqk,khd->hqd",
        local_probs.astype(jnp.bfloat16),
        value_all,
        preferred_element_type=jnp.float32,
    )
    head_index = jnp.arange(HEADS)

    def pick_block(field, block_index):
        return field.reshape(block_rate, BLOCK, HEADS, HEAD_DIM)[block_index, :, head_index, :]

    near_pair = (pick_block(key_all, near_offset), pick_block(value_all, near_offset))
    far_class = far_offset // block_rate
    far_block = far_offset % block_rate
    far_pair = (pick_block(key_all, far_block), pick_block(value_all, far_block))
    near_position = jnp.where(seq_index < half_size, seq_index, (seq_index - half_size) % near_size)
    far_position = seq_index // STRIDE % far_size
    near_keys, near_values, near_distance = near_shifts(near_pair, near_size, near_position)
    far_keys, far_values, far_distance = far_shifts(far_pair, far_size, far_position)
    near_top, near_sum, near_out = level_stats(
        pick_block(query, near_offset), near_keys, near_values, near_distance
    )
    far_top, far_sum, far_out = level_stats(
        pick_block(query, far_block), far_keys, far_values, far_distance
    )

    def spread_rows(field):
        widened = jnp.broadcast_to(field[:, None], (HEADS, block_rate) + field.shape[1:])
        return widened.reshape((HEADS, row_count) + field.shape[2:])

    near_mask = jnp.arange(block_rate)[None, :] == near_offset[:, None]
    far_mask = (jnp.arange(block_rate)[None, :] == far_block[:, None]) & (
        seq_index % STRIDE == far_class
    )[:, None]
    near_mask_rows = jnp.broadcast_to(near_mask[:, :, None], (HEADS, block_rate, BLOCK)).reshape(
        HEADS, row_count
    )
    far_mask_rows = jnp.broadcast_to(far_mask[:, :, None], (HEADS, block_rate, BLOCK)).reshape(
        HEADS, row_count
    )
    near_top_rows = jnp.where(near_mask_rows, spread_rows(near_top), NEG)
    far_top_rows = jnp.where(far_mask_rows, spread_rows(far_top), NEG)
    best_score = jnp.maximum(jnp.maximum(local_top, near_top_rows), far_top_rows)
    local_weight = jnp.exp(local_top - best_score)
    near_weight = jnp.where(near_mask_rows, jnp.exp(near_top_rows - best_score), 0.0)
    far_weight = jnp.where(far_mask_rows, jnp.exp(far_top_rows - best_score), 0.0)
    numerator = (
        local_weight[..., None] * local_out
        + near_weight[..., None] * spread_rows(near_out)
        + far_weight[..., None] * spread_rows(far_out)
    )
    denominator = (
        local_weight * local_sum
        + near_weight * spread_rows(near_sum)
        + far_weight * spread_rows(far_sum)
    )
    mixed = numerator / denominator[..., None]
    return mixed.transpose(1, 0, 2).reshape(1, row_count, qkv_width).astype(jnp.bfloat16)


def solution(mesh):
    in_specs = (P("fsdp", "seq", None), P("fsdp", None), P(), P())
    out_specs = P("fsdp", "seq", None)
    return jax.shard_map(body, mesh=mesh, in_specs=in_specs, out_specs=out_specs, check_vma=False)
```

profile of v0, /device:TPU:385, one launch (start us, length us, event | category | flops | bytes accessed | tf_op | source)
XLA Modules:
  0.0 676.8 jit_solution(2399034957391750225)
XLA Ops:
  9.8 73.1 %all-gather.2.cloned.1.call-done = bf16[2048,1536]{1,0:T(8,128)(2,1)} async-done(((bf16[512,1536]{1,0:T(8,128)(2,1)}), bf16[2048,1536]{1,0:T(8,128)(2,1)}) %all-gather.2.cloned.1.call-update) | async-done | bytes 6291472 | tf_op jit(solution)/shard_map/all_gather | solution.py:92
  83.0 6.2 convolution_convert_fusion
  136.0 53.3 %collective-permute-done.48 = bf16[4,128,128]{2,1,0:T(8,128)(2,1)S(1)} collective-permute-done((bf16[4,128,128]{2,1,0:T(8,128)(2,1)}, bf16[4,128,128]{2,1,0:T(8,128)(2,1)S(1)}, u32[]{:S(2)}, u32[]{:S(2)}) %collective-permute-start.48) | collective-permute-done | bytes 131104 | tf_op jit(solution)/shard_map/ppermute | solution.py:18
  191.9 15.0 %collective-permute-done.50 = bf16[4,128,128]{2,1,0:T(8,128)(2,1)S(1)} collective-permute-done((bf16[4,128,128]{2,1,0:T(8,128)(2,1)}, bf16[4,128,128]{2,1,0:T(8,128)(2,1)S(1)}, u32[]{:S(2)}, u32[]{:S(2)}) %collective-permute-start.50) | collective-permute-done | bytes 131104 | tf_op jit(solution)/shard_map/ppermute | solution.py:18
  209.5 12.2 %collective-permute-done.52 = bf16[4,128,128]{2,1,0:T(8,128)(2,1)S(1)} collective-permute-done((bf16[4,128,128]{2,1,0:T(8,128)(2,1)}, bf16[4,128,128]{2,1,0:T(8,128)(2,1)S(1)}, u32[]{:S(2)}, u32[]{:S(2)}) %collective-permute-start.52) | collective-permute-done | bytes 131104 | tf_op jit(solution)/shard_map/ppermute | solution.py:18
  224.4 18.9 %collective-permute-done.54 = bf16[4,128,128]{2,1,0:T(8,128)(2,1)S(1)} collective-permute-done((bf16[4,128,128]{2,1,0:T(8,128)(2,1)}, bf16[4,128,128]{2,1,0:T(8,128)(2,1)S(1)}, u32[]{:S(2)}, u32[]{:S(2)}) %collective-permute-start.54) | collective-permute-done | bytes 131104 | tf_op jit(solution)/shard_map/ppermute | solution.py:18
  244.5 6.1 collective-permute-done.55
  252.6 6.5 collective-permute-done.56
  261.9 12.8 %collective-permute-done.57 = bf16[4,128,128]{2,1,0:T(8,128)(2,1)S(1)} collective-permute-done((bf16[4,128,128]{2,1,0:T(8,128)(2,1)}, bf16[4,128,128]{2,1,0:T(8,128)(2,1)S(1)}, u32[]{:S(2)}, u32[]{:S(2)}) %collective-permute-start.57) | collective-permute-done | bytes 131104 | tf_op jit(solution)/shard_map/ppermute | solution.py:18
  274.7 7.9 %collective-permute-start.59 = (bf16[4,128,128]{2,1,0:T(8,128)(2,1)}, bf16[4,128,128]{2,1,0:T(8,128)(2,1)S(1)}, u32[]{:S(2)}, u32[]{:S(2)}) collective-permute-start(bf16[4,128,128]{2,1,0:T(8,128)(2,1)} %gather_fusion.5), channel_id=1, source_target_pairs={{0,32},{4,36},{8,40},{12,44},{16,48},{20,52},{24,56},{28,60},{32,6... | collective-permute-start | bytes 393224 | tf_op jit(solution)/shard_map/ppermute | solution.py:18
  282.6 12.0 %collective-permute-start.31 = (bf16[4,128,128]{2,1,0:T(8,128)(2,1)S(1)}, bf16[4,128,128]{2,1,0:T(8,128)(2,1)S(1)}, u32[]{:S(2)}, u32[]{:S(2)}) collective-permute-start(bf16[4,128,128]{2,1,0:T(8,128)(2,1)S(1)} %gather_fusion.4), channel_id=1, source_target_pairs={{0,56},{4,60},{8,64},{12,68},{16,72},{20,76},{24,80},{28,84},{32,8... | collective-permute-start | bytes 393224 | tf_op jit(solution)/shard_map/ppermute | solution.py:18
  296.9 8.1 %collective-permute-start.30 = (bf16[4,128,128]{2,1,0:T(8,128)(2,1)S(1)}, bf16[4,128,128]{2,1,0:T(8,128)(2,1)S(1)}, u32[]{:S(2)}, u32[]{:S(2)}) collective-permute-start(bf16[4,128,128]{2,1,0:T(8,128)(2,1)S(1)} %gather_fusion.4), channel_id=1, source_target_pairs={{0,60},{4,64},{8,68},{12,72},{16,76},{20,80},{24,84},{28,88},{32,9... | collective-permute-start | bytes 393224 | tf_op jit(solution)/shard_map/ppermute | solution.py:18
  306.0 9.7 %collective-permute-done.30 = bf16[4,128,128]{2,1,0:T(8,128)(2,1)S(1)} collective-permute-done((bf16[4,128,128]{2,1,0:T(8,128)(2,1)S(1)}, bf16[4,128,128]{2,1,0:T(8,128)(2,1)S(1)}, u32[]{:S(2)}, u32[]{:S(2)}) %collective-permute-start.30) | collective-permute-done | bytes 131104 | tf_op jit(solution)/shard_map/ppermute | solution.py:18
  315.6 4.9 collective-permute-start.32
  322.5 8.1 %collective-permute-done.32 = bf16[4,128,128]{2,1,0:T(8,128)(2,1)S(1)} collective-permute-done((bf16[4,128,128]{2,1,0:T(8,128)(2,1)S(1)}, bf16[4,128,128]{2,1,0:T(8,128)(2,1)S(1)}, u32[]{:S(2)}, u32[]{:S(2)}) %collective-permute-start.32) | collective-permute-done | bytes 131104 | tf_op jit(solution)/shard_map/ppermute | solution.py:18
  332.5 5.8 collective-permute-done.33
  344.2 7.6 %collective-permute-done.35 = bf16[4,128,128]{2,1,0:T(8,128)(2,1)S(1)} collective-permute-done((bf16[4,128,128]{2,1,0:T(8,128)(2,1)S(1)}, bf16[4,128,128]{2,1,0:T(8,128)(2,1)S(1)}, u32[]{:S(2)}, u32[]{:S(2)}) %collective-permute-start.35) | collective-permute-done | bytes 131104 | tf_op jit(solution)/shard_map/ppermute | solution.py:18
  391.9 35.4 %collective-permute-done.18 = bf16[4,128,128]{2,1,0:T(8,128)(2,1)S(1)} collective-permute-done((bf16[4,128,128]{2,1,0:T(8,128)(2,1)S(1)}, bf16[4,128,128]{2,1,0:T(8,128)(2,1)S(1)}, u32[]{:S(2)}, u32[]{:S(2)}) %collective-permute-start.18) | collective-permute-done | bytes 131104 | tf_op jit(solution)/shard_map/ppermute | solution.py:18
  429.9 17.6 %collective-permute-done.20 = bf16[4,128,128]{2,1,0:T(8,128)(2,1)S(1)} collective-permute-done((bf16[4,128,128]{2,1,0:T(8,128)(2,1)S(1)}, bf16[4,128,128]{2,1,0:T(8,128)(2,1)S(1)}, u32[]{:S(2)}, u32[]{:S(2)}) %collective-permute-start.20) | collective-permute-done | bytes 131104 | tf_op jit(solution)/shard_map/ppermute | solution.py:18
  450.1 11.9 %collective-permute-done.22 = bf16[4,128,128]{2,1,0:T(8,128)(2,1)S(1)} collective-permute-done((bf16[4,128,128]{2,1,0:T(8,128)(2,1)S(1)}, bf16[4,128,128]{2,1,0:T(8,128)(2,1)S(1)}, u32[]{:S(2)}, u32[]{:S(2)}) %collective-permute-start.22) | collective-permute-done | bytes 131104 | tf_op jit(solution)/shard_map/ppermute | solution.py:18
  466.2 10.0 %collective-permute-done.24 = bf16[4,128,128]{2,1,0:T(8,128)(2,1)S(1)} collective-permute-done((bf16[4,128,128]{2,1,0:T(8,128)(2,1)S(1)}, bf16[4,128,128]{2,1,0:T(8,128)(2,1)S(1)}, u32[]{:S(2)}, u32[]{:S(2)}) %collective-permute-start.24) | collective-permute-done | bytes 131104 | tf_op jit(solution)/shard_map/ppermute | solution.py:18
  477.5 12.3 %collective-permute-done.25 = bf16[4,128,128]{2,1,0:T(8,128)(2,1)S(1)} collective-permute-done((bf16[4,128,128]{2,1,0:T(8,128)(2,1)S(1)}, bf16[4,128,128]{2,1,0:T(8,128)(2,1)S(1)}, u32[]{:S(2)}, u32[]{:S(2)}) %collective-permute-start.25) | collective-permute-done | bytes 131104 | tf_op jit(solution)/shard_map/ppermute | solution.py:18
  489.8 16.5 %collective-permute-start.27 = (bf16[4,128,128]{2,1,0:T(8,128)(2,1)S(1)}, bf16[4,128,128]{2,1,0:T(8,128)(2,1)S(1)}, u32[]{:S(2)}, u32[]{:S(2)}) collective-permute-start(bf16[4,128,128]{2,1,0:T(8,128)(2,1)S(1)} %gather_fusion.3), channel_id=1, source_target_pairs={{0,96},{4,100},{8,104},{12,108},{16,112},{20,116},{24,120},{28,124... | collective-permute-start | bytes 393224 | tf_op jit(solution)/shard_map/ppermute | solution.py:18
  508.3 17.3 %collective-permute-done.27 = bf16[4,128,128]{2,1,0:T(8,128)(2,1)S(1)} collective-permute-done((bf16[4,128,128]{2,1,0:T(8,128)(2,1)S(1)}, bf16[4,128,128]{2,1,0:T(8,128)(2,1)S(1)}, u32[]{:S(2)}, u32[]{:S(2)}) %collective-permute-start.27) | collective-permute-done | bytes 131104 | tf_op jit(solution)/shard_map/ppermute | solution.py:18
  527.5 14.9 %collective-permute-start.1 = (bf16[4,128,128]{2,1,0:T(8,128)(2,1)}, bf16[4,128,128]{2,1,0:T(8,128)(2,1)S(1)}, u32[]{:S(2)}, u32[]{:S(2)}) collective-permute-start(bf16[4,128,128]{2,1,0:T(8,128)(2,1)} %gather_fusion.1), channel_id=1, source_target_pairs={{0,56},{4,60},{8,64},{12,68},{16,72},{20,76},{24,80},{28,84},{32,8... | collective-permute-start | bytes 393224 | tf_op jit(solution)/shard_map/ppermute | solution.py:18
  542.5 21.1 %collective-permute-start = (bf16[4,128,128]{2,1,0:T(8,128)(2,1)}, bf16[4,128,128]{2,1,0:T(8,128)(2,1)S(1)}, u32[]{:S(2)}, u32[]{:S(2)}) collective-permute-start(bf16[4,128,128]{2,1,0:T(8,128)(2,1)} %gather_fusion.1), channel_id=1, source_target_pairs={{0,60},{4,64},{8,68},{12,72},{16,76},{20,80},{24,84},{28,88},{32,9... | collective-permute-start | bytes 393224 | tf_op jit(solution)/shard_map/ppermute | solution.py:18
  563.7 13.4 %collective-permute-done = bf16[4,128,128]{2,1,0:T(8,128)(2,1)S(1)} collective-permute-done((bf16[4,128,128]{2,1,0:T(8,128)(2,1)}, bf16[4,128,128]{2,1,0:T(8,128)(2,1)S(1)}, u32[]{:S(2)}, u32[]{:S(2)}) %collective-permute-start) | collective-permute-done | bytes 131104 | tf_op jit(solution)/shard_map/ppermute | solution.py:18
  581.0 9.0 %collective-permute-done.2 = bf16[4,128,128]{2,1,0:T(8,128)(2,1)S(1)} collective-permute-done((bf16[4,128,128]{2,1,0:T(8,128)(2,1)}, bf16[4,128,128]{2,1,0:T(8,128)(2,1)S(1)}, u32[]{:S(2)}, u32[]{:S(2)}) %collective-permute-start.2) | collective-permute-done | bytes 131104 | tf_op jit(solution)/shard_map/ppermute | solution.py:18
  592.5 14.3 %collective-permute-done.3 = bf16[4,128,128]{2,1,0:T(8,128)(2,1)S(1)} collective-permute-done((bf16[4,128,128]{2,1,0:T(8,128)(2,1)}, bf16[4,128,128]{2,1,0:T(8,128)(2,1)S(1)}, u32[]{:S(2)}, u32[]{:S(2)}) %collective-permute-start.3) | collective-permute-done | bytes 131104 | tf_op jit(solution)/shard_map/ppermute | solution.py:18
  610.8 9.5 %collective-permute-done.5 = bf16[4,128,128]{2,1,0:T(8,128)(2,1)S(1)} collective-permute-done((bf16[4,128,128]{2,1,0:T(8,128)(2,1)}, bf16[4,128,128]{2,1,0:T(8,128)(2,1)S(1)}, u32[]{:S(2)}, u32[]{:S(2)}) %collective-permute-start.5) | collective-permute-done | bytes 131104 | tf_op jit(solution)/shard_map/ppermute | solution.py:18
  641.0 6.5 collective-permute-done.11
  664.6 4.4 divide_convert_fusion
  (231 shorter events, 179.7 us)
Async XLA Ops:
  6.5 76.4 %all-gather.2.cloned.1.call-start = ((), (), s32[]{:S(2)}) async-start(), calls=%async_computation | async-start | bytes 7864320 | tf_op jit(solution)/shard_map/all_gather | solution.py:92
  96.7 552.6 %collective-permute-start.14 = (bf16[4,128,128]{2,1,0:T(8,128)(2,1)}, bf16[4,128,128]{2,1,0:T(8,128)(2,1)}, u32[]{:S(2)}, u32[]{:S(2)}) collective-permute-start(bf16[4,128,128]{2,1,0:T(8,128)(2,1)} %gather_fusion.1), channel_id=1, source_target_pairs={{0,4},{4,8},{8,12},{12,16},{16,20},{20,24},{24,28},{28,32},{32,36}... | collective-permute-start | bytes 393224 | tf_op jit(solution)/shard_map/ppermute | solution.py:18
  100.4 547.1 %collective-permute-start.12 = (bf16[4,128,128]{2,1,0:T(8,128)(2,1)}, bf16[4,128,128]{2,1,0:T(8,128)(2,1)}, u32[]{:S(2)}, u32[]{:S(2)}) collective-permute-start(bf16[4,128,128]{2,1,0:T(8,128)(2,1)} %gather_fusion.1), channel_id=1, source_target_pairs={{0,12},{4,16},{8,20},{12,24},{16,28},{20,32},{24,36},{28,40},{32,4... | collective-permute-start | bytes 393224 | tf_op jit(solution)/shard_map/ppermute | solution.py:18
  109.0 23.4 %collective-permute-start.46 = (bf16[4,128,128]{2,1,0:T(8,128)(2,1)}, bf16[4,128,128]{2,1,0:T(8,128)(2,1)}, u32[]{:S(2)}, u32[]{:S(2)}) collective-permute-start(bf16[4,128,128]{2,1,0:T(8,128)(2,1)} %gather_fusion.5), channel_id=1, source_target_pairs={{0,448},{4,452},{8,456},{12,460},{16,464},{20,468},{24,472},{28,47... | collective-permute-start | bytes 393224 | tf_op jit(solution)/shard_map/ppermute | solution.py:18
  110.3 20.5 %collective-permute-start.45 = (bf16[4,128,128]{2,1,0:T(8,128)(2,1)}, bf16[4,128,128]{2,1,0:T(8,128)(2,1)}, u32[]{:S(2)}, u32[]{:S(2)}) collective-permute-start(bf16[4,128,128]{2,1,0:T(8,128)(2,1)} %gather_fusion.5), channel_id=1, source_target_pairs={{0,480},{4,484},{8,488},{12,492},{16,496},{20,500},{24,504},{28,50... | collective-permute-start | bytes 393224 | tf_op jit(solution)/shard_map/ppermute | solution.py:18
  118.8 529.6 %collective-permute-start.13 = (bf16[4,128,128]{2,1,0:T(8,128)(2,1)}, bf16[4,128,128]{2,1,0:T(8,128)(2,1)}, u32[]{:S(2)}, u32[]{:S(2)}) collective-permute-start(bf16[4,128,128]{2,1,0:T(8,128)(2,1)} %gather_fusion.1), channel_id=1, source_target_pairs={{0,8},{4,12},{8,16},{12,20},{16,24},{20,28},{24,32},{28,36},{32,40... | collective-permute-start | bytes 393224 | tf_op jit(solution)/shard_map/ppermute | solution.py:18
  132.4 56.9 %collective-permute-start.48 = (bf16[4,128,128]{2,1,0:T(8,128)(2,1)}, bf16[4,128,128]{2,1,0:T(8,128)(2,1)S(1)}, u32[]{:S(2)}, u32[]{:S(2)}) collective-permute-start(bf16[4,128,128]{2,1,0:T(8,128)(2,1)} %gather_fusion.5), channel_id=1, source_target_pairs={{0,384},{4,388},{8,392},{12,396},{16,400},{20,404},{24,408},{28,41... | collective-permute-start | bytes 393224 | tf_op jit(solution)/shard_map/ppermute | solution.py:18
  134.7 55.9 %collective-permute-start.49 = (bf16[4,128,128]{2,1,0:T(8,128)(2,1)}, bf16[4,128,128]{2,1,0:T(8,128)(2,1)S(1)}, u32[]{:S(2)}, u32[]{:S(2)}) collective-permute-start(bf16[4,128,128]{2,1,0:T(8,128)(2,1)} %gather_fusion.5), channel_id=1, source_target_pairs={{0,352},{4,356},{8,360},{12,364},{16,368},{20,372},{24,376},{28,38... | collective-permute-start | bytes 393224 | tf_op jit(solution)/shard_map/ppermute | solution.py:18
  189.3 17.6 %collective-permute-start.50 = (bf16[4,128,128]{2,1,0:T(8,128)(2,1)}, bf16[4,128,128]{2,1,0:T(8,128)(2,1)S(1)}, u32[]{:S(2)}, u32[]{:S(2)}) collective-permute-start(bf16[4,128,128]{2,1,0:T(8,128)(2,1)} %gather_fusion.5), channel_id=1, source_target_pairs={{0,320},{4,324},{8,328},{12,332},{16,336},{20,340},{24,344},{28,34... | collective-permute-start | bytes 393224 | tf_op jit(solution)/shard_map/ppermute | solution.py:18
  190.6 17.6 %collective-permute-start.51 = (bf16[4,128,128]{2,1,0:T(8,128)(2,1)}, bf16[4,128,128]{2,1,0:T(8,128)(2,1)S(1)}, u32[]{:S(2)}, u32[]{:S(2)}) collective-permute-start(bf16[4,128,128]{2,1,0:T(8,128)(2,1)} %gather_fusion.5), channel_id=1, source_target_pairs={{0,288},{4,292},{8,296},{12,300},{16,304},{20,308},{24,312},{28,31... | collective-permute-start | bytes 393224 | tf_op jit(solution)/shard_map/ppermute | solution.py:18
  221.7 21.5 %collective-permute-start.54 = (bf16[4,128,128]{2,1,0:T(8,128)(2,1)}, bf16[4,128,128]{2,1,0:T(8,128)(2,1)S(1)}, u32[]{:S(2)}, u32[]{:S(2)}) collective-permute-start(bf16[4,128,128]{2,1,0:T(8,128)(2,1)} %gather_fusion.5), channel_id=1, source_target_pairs={{0,192},{4,196},{8,200},{12,204},{16,208},{20,212},{24,216},{28,22... | collective-permute-start | bytes 393224 | tf_op jit(solution)/shard_map/ppermute | solution.py:18
  223.0 27.6 %collective-permute-start.55 = (bf16[4,128,128]{2,1,0:T(8,128)(2,1)}, bf16[4,128,128]{2,1,0:T(8,128)(2,1)S(1)}, u32[]{:S(2)}, u32[]{:S(2)}) collective-permute-start(bf16[4,128,128]{2,1,0:T(8,128)(2,1)} %gather_fusion.5), channel_id=1, source_target_pairs={{0,160},{4,164},{8,168},{12,172},{16,176},{20,180},{24,184},{28,18... | collective-permute-start | bytes 393224 | tf_op jit(solution)/shard_map/ppermute | solution.py:18
  250.7 24.0 %collective-permute-start.57 = (bf16[4,128,128]{2,1,0:T(8,128)(2,1)}, bf16[4,128,128]{2,1,0:T(8,128)(2,1)S(1)}, u32[]{:S(2)}, u32[]{:S(2)}) collective-permute-start(bf16[4,128,128]{2,1,0:T(8,128)(2,1)} %gather_fusion.5), channel_id=1, source_target_pairs={{0,96},{4,100},{8,104},{12,108},{16,112},{20,116},{24,120},{28,124... | collective-permute-start | bytes 393224 | tf_op jit(solution)/shard_map/ppermute | solution.py:18
  259.2 23.5 %collective-permute-start.58 = (bf16[4,128,128]{2,1,0:T(8,128)(2,1)}, bf16[4,128,128]{2,1,0:T(8,128)(2,1)S(1)}, u32[]{:S(2)}, u32[]{:S(2)}) collective-permute-start(bf16[4,128,128]{2,1,0:T(8,128)(2,1)} %gather_fusion.5), channel_id=1, source_target_pairs={{0,64},{4,68},{8,72},{12,76},{16,80},{20,84},{24,88},{28,92},{32,9... | collective-permute-start | bytes 393224 | tf_op jit(solution)/shard_map/ppermute | solution.py:18
  274.7 22.2 %collective-permute-start.59 = (bf16[4,128,128]{2,1,0:T(8,128)(2,1)}, bf16[4,128,128]{2,1,0:T(8,128)(2,1)S(1)}, u32[]{:S(2)}, u32[]{:S(2)}) collective-permute-start(bf16[4,128,128]{2,1,0:T(8,128)(2,1)} %gather_fusion.5), channel_id=1, source_target_pairs={{0,32},{4,36},{8,40},{12,44},{16,48},{20,52},{24,56},{28,60},{32,6... | collective-permute-start | bytes 393224 | tf_op jit(solution)/shard_map/ppermute | solution.py:18
  282.6 37.9 %collective-permute-start.31 = (bf16[4,128,128]{2,1,0:T(8,128)(2,1)S(1)}, bf16[4,128,128]{2,1,0:T(8,128)(2,1)S(1)}, u32[]{:S(2)}, u32[]{:S(2)}) collective-permute-start(bf16[4,128,128]{2,1,0:T(8,128)(2,1)S(1)} %gather_fusion.4), channel_id=1, source_target_pairs={{0,56},{4,60},{8,64},{12,68},{16,72},{20,76},{24,80},{28,84},{32,8... | collective-permute-start | bytes 393224 | tf_op jit(solution)/shard_map/ppermute | solution.py:18
  296.9 18.7 %collective-permute-start.30 = (bf16[4,128,128]{2,1,0:T(8,128)(2,1)S(1)}, bf16[4,128,128]{2,1,0:T(8,128)(2,1)S(1)}, u32[]{:S(2)}, u32[]{:S(2)}) collective-permute-start(bf16[4,128,128]{2,1,0:T(8,128)(2,1)S(1)} %gather_fusion.4), channel_id=1, source_target_pairs={{0,60},{4,64},{8,68},{12,72},{16,76},{20,80},{24,84},{28,88},{32,9... | collective-permute-start | bytes 393224 | tf_op jit(solution)/shard_map/ppermute | solution.py:18
  320.5 17.8 %collective-permute-start.33 = (bf16[4,128,128]{2,1,0:T(8,128)(2,1)S(1)}, bf16[4,128,128]{2,1,0:T(8,128)(2,1)S(1)}, u32[]{:S(2)}, u32[]{:S(2)}) collective-permute-start(bf16[4,128,128]{2,1,0:T(8,128)(2,1)S(1)} %gather_fusion.4), channel_id=1, source_target_pairs={{0,48},{4,52},{8,56},{12,60},{16,64},{20,68},{24,72},{28,76},{32,8... | collective-permute-start | bytes 393224 | tf_op jit(solution)/shard_map/ppermute | solution.py:18
  389.2 38.0 %collective-permute-start.18 = (bf16[4,128,128]{2,1,0:T(8,128)(2,1)S(1)}, bf16[4,128,128]{2,1,0:T(8,128)(2,1)S(1)}, u32[]{:S(2)}, u32[]{:S(2)}) collective-permute-start(bf16[4,128,128]{2,1,0:T(8,128)(2,1)S(1)} %gather_fusion.3), channel_id=1, source_target_pairs={{0,384},{4,388},{8,392},{12,396},{16,400},{20,404},{24,408},{28,41... | collective-permute-start | bytes 393224 | tf_op jit(solution)/shard_map/ppermute | solution.py:18
  390.6 38.0 %collective-permute-start.19 = (bf16[4,128,128]{2,1,0:T(8,128)(2,1)S(1)}, bf16[4,128,128]{2,1,0:T(8,128)(2,1)S(1)}, u32[]{:S(2)}, u32[]{:S(2)}) collective-permute-start(bf16[4,128,128]{2,1,0:T(8,128)(2,1)S(1)} %gather_fusion.3), channel_id=1, source_target_pairs={{0,352},{4,356},{8,360},{12,364},{16,368},{20,372},{24,376},{28,38... | collective-permute-start | bytes 393224 | tf_op jit(solution)/shard_map/ppermute | solution.py:18
  427.3 20.2 %collective-permute-start.20 = (bf16[4,128,128]{2,1,0:T(8,128)(2,1)S(1)}, bf16[4,128,128]{2,1,0:T(8,128)(2,1)S(1)}, u32[]{:S(2)}, u32[]{:S(2)}) collective-permute-start(bf16[4,128,128]{2,1,0:T(8,128)(2,1)S(1)} %gather_fusion.3), channel_id=1, source_target_pairs={{0,320},{4,324},{8,328},{12,332},{16,336},{20,340},{24,344},{28,34... | collective-permute-start | bytes 393224 | tf_op jit(solution)/shard_map/ppermute | solution.py:18
  428.6 20.2 %collective-permute-start.21 = (bf16[4,128,128]{2,1,0:T(8,128)(2,1)S(1)}, bf16[4,128,128]{2,1,0:T(8,128)(2,1)S(1)}, u32[]{:S(2)}, u32[]{:S(2)}) collective-permute-start(bf16[4,128,128]{2,1,0:T(8,128)(2,1)S(1)} %gather_fusion.3), channel_id=1, source_target_pairs={{0,288},{4,292},{8,296},{12,300},{16,304},{20,308},{24,312},{28,31... | collective-permute-start | bytes 393224 | tf_op jit(solution)/shard_map/ppermute | solution.py:18
  448.8 16.0 %collective-permute-start.23 = (bf16[4,128,128]{2,1,0:T(8,128)(2,1)S(1)}, bf16[4,128,128]{2,1,0:T(8,128)(2,1)S(1)}, u32[]{:S(2)}, u32[]{:S(2)}) collective-permute-start(bf16[4,128,128]{2,1,0:T(8,128)(2,1)S(1)} %gather_fusion.3), channel_id=1, source_target_pairs={{0,224},{4,228},{8,232},{12,236},{16,240},{20,244},{24,248},{28,25... | collective-permute-start | bytes 393224 | tf_op jit(solution)/shard_map/ppermute | solution.py:18
  464.9 24.9 %collective-permute-start.25 = (bf16[4,128,128]{2,1,0:T(8,128)(2,1)S(1)}, bf16[4,128,128]{2,1,0:T(8,128)(2,1)S(1)}, u32[]{:S(2)}, u32[]{:S(2)}) collective-permute-start(bf16[4,128,128]{2,1,0:T(8,128)(2,1)S(1)} %gather_fusion.3), channel_id=1, source_target_pairs={{0,160},{4,164},{8,168},{12,172},{16,176},{20,180},{24,184},{28,18... | collective-permute-start | bytes 393224 | tf_op jit(solution)/shard_map/ppermute | solution.py:18
  476.2 30.1 %collective-permute-start.26 = (bf16[4,128,128]{2,1,0:T(8,128)(2,1)S(1)}, bf16[4,128,128]{2,1,0:T(8,128)(2,1)S(1)}, u32[]{:S(2)}, u32[]{:S(2)}) collective-permute-start(bf16[4,128,128]{2,1,0:T(8,128)(2,1)S(1)} %gather_fusion.3), channel_id=1, source_target_pairs={{0,128},{4,132},{8,136},{12,140},{16,144},{20,148},{24,152},{28,15... | collective-permute-start | bytes 393224 | tf_op jit(solution)/shard_map/ppermute | solution.py:18
  489.8 35.8 %collective-permute-start.27 = (bf16[4,128,128]{2,1,0:T(8,128)(2,1)S(1)}, bf16[4,128,128]{2,1,0:T(8,128)(2,1)S(1)}, u32[]{:S(2)}, u32[]{:S(2)}) collective-permute-start(bf16[4,128,128]{2,1,0:T(8,128)(2,1)S(1)} %gather_fusion.3), channel_id=1, source_target_pairs={{0,96},{4,100},{8,104},{12,108},{16,112},{20,116},{24,120},{28,124... | collective-permute-start | bytes 393224 | tf_op jit(solution)/shard_map/ppermute | solution.py:18
  506.3 21.2 %collective-permute-start.28 = (bf16[4,128,128]{2,1,0:T(8,128)(2,1)S(1)}, bf16[4,128,128]{2,1,0:T(8,128)(2,1)S(1)}, u32[]{:S(2)}, u32[]{:S(2)}) collective-permute-start(bf16[4,128,128]{2,1,0:T(8,128)(2,1)S(1)} %gather_fusion.3), channel_id=1, source_target_pairs={{0,64},{4,68},{8,72},{12,76},{16,80},{20,84},{24,88},{28,92},{32,9... | collective-permute-start | bytes 393224 | tf_op jit(solution)/shard_map/ppermute | solution.py:18
  525.6 16.9 %collective-permute-start.29 = (bf16[4,128,128]{2,1,0:T(8,128)(2,1)S(1)}, bf16[4,128,128]{2,1,0:T(8,128)(2,1)S(1)}, u32[]{:S(2)}, u32[]{:S(2)}) collective-permute-start(bf16[4,128,128]{2,1,0:T(8,128)(2,1)S(1)} %gather_fusion.3), channel_id=1, source_target_pairs={{0,32},{4,36},{8,40},{12,44},{16,48},{20,52},{24,56},{28,60},{32,6... | collective-permute-start | bytes 393224 | tf_op jit(solution)/shard_map/ppermute | solution.py:18
  527.5 51.5 %collective-permute-start.1 = (bf16[4,128,128]{2,1,0:T(8,128)(2,1)}, bf16[4,128,128]{2,1,0:T(8,128)(2,1)S(1)}, u32[]{:S(2)}, u32[]{:S(2)}) collective-permute-start(bf16[4,128,128]{2,1,0:T(8,128)(2,1)} %gather_fusion.1), channel_id=1, source_target_pairs={{0,56},{4,60},{8,64},{12,68},{16,72},{20,76},{24,80},{28,84},{32,8... | collective-permute-start | bytes 393224 | tf_op jit(solution)/shard_map/ppermute | solution.py:18
  542.5 34.6 %collective-permute-start = (bf16[4,128,128]{2,1,0:T(8,128)(2,1)}, bf16[4,128,128]{2,1,0:T(8,128)(2,1)S(1)}, u32[]{:S(2)}, u32[]{:S(2)}) collective-permute-start(bf16[4,128,128]{2,1,0:T(8,128)(2,1)} %gather_fusion.1), channel_id=1, source_target_pairs={{0,60},{4,64},{8,68},{12,72},{16,76},{20,80},{24,84},{28,88},{32,9... | collective-permute-start | bytes 393224 | tf_op jit(solution)/shard_map/ppermute | solution.py:18
  579.1 27.8 %collective-permute-start.3 = (bf16[4,128,128]{2,1,0:T(8,128)(2,1)}, bf16[4,128,128]{2,1,0:T(8,128)(2,1)S(1)}, u32[]{:S(2)}, u32[]{:S(2)}) collective-permute-start(bf16[4,128,128]{2,1,0:T(8,128)(2,1)} %gather_fusion.1), channel_id=1, source_target_pairs={{0,48},{4,52},{8,56},{12,60},{16,64},{20,68},{24,72},{28,76},{32,8... | collective-permute-start | bytes 393224 | tf_op jit(solution)/shard_map/ppermute | solution.py:18
  590.0 18.8 %collective-permute-start.4 = (bf16[4,128,128]{2,1,0:T(8,128)(2,1)}, bf16[4,128,128]{2,1,0:T(8,128)(2,1)S(1)}, u32[]{:S(2)}, u32[]{:S(2)}) collective-permute-start(bf16[4,128,128]{2,1,0:T(8,128)(2,1)} %gather_fusion.1), channel_id=1, source_target_pairs={{0,44},{4,48},{8,52},{12,56},{16,60},{20,64},{24,68},{28,72},{32,7... | collective-permute-start | bytes 393224 | tf_op jit(solution)/shard_map/ppermute | solution.py:18
  (42 other events, 642.6 us)
Sparse Core Ops, SparseCore 0:
  9.5 73.4 all-gather.1
where the time goes:
time: 679 us; the launch traced here: 677 us
  waiting for transfers between devices  422 us (62%)
  starting transfers between devices  175 us (26%)
  local copies, waits for them, and re-layouts  40.5 us (6%)
  matrix products  19.3 us (3%)
  between operations  15 us (2%)
    ppermute x60, waiting for transfers between devices, from_behind(): lax.ppermute(value, axis, [(source, source + steps) for source in range(f...  348 us
    ppermute x60, starting transfers between devices, from_behind(): lax.ppermute(value, axis, [(source, source + steps) for source in range(f...  175 us
    all_gather x1, waiting for transfers between devices, body(): lax.all_gather(qkv_weight, 'fsdp', axis=0, tiled=True)  73.1 us
  transfers between devices with their start and end apart: 61, of which 37 were waited for; matrix products, arithmetic and copies ran while one was open for 4% of the time, Pallas kernels for 0%

commit v1 on v0

v1 whole, which is shorter than its diff:
```python
import jax
import jax.numpy as jnp
from jax import lax
from jax.experimental import pallas as pl
from jax.experimental.pallas import tpu as pltpu
from jax.sharding import PartitionSpec as P

HEADS = 4
HD = 128
NZ = 16
SCALE = HD ** (-0.5)
NEG = -1e30
BF = jnp.bfloat16
F32 = jnp.float32

X_DIR, X_FWD, Y_W, Z_W, C_W = 0, 4, 8, 11, 14
F_SIB, F_PLANE, N_Q, N_KV, N_SIB, N_UP, N_UPSIB = 26, 27, 30, 33, 36, 37, 38
R_UP, R_DN, N_O, N_L, F_O, F_L = 39, 47, 54, 57, 60, 67
N_SEM = 74


def qk(q, k):
    return lax.dot_general(q, k, (((1,), (1,)), ((), ())), preferred_element_type=F32) * SCALE


def pv(p, v):
    return jnp.dot(p.astype(BF), v, preferred_element_type=F32)


def lanes(column):
    return jnp.broadcast_to(column, (128, 128))


def kernel(tok, wgt, noff, foff, out, wfull, tokv, acc, proj, fa_snd, fa_rcv, fsel, fcand, kvf,
           nqs, nks, nq, nkv, ncross, nm, nl, no, nos, nls, nor, nlr, fos, fls, fo, fl, lo, ll,
           ssem, rsem, lsem):
    seq = lax.axis_index("seq")
    x = lax.axis_index("fsdp")
    z = lax.div(seq, 8)
    y = lax.rem(lax.div(seq, 2), 4)
    c = lax.rem(seq, 2)
    oc = 1 - c

    def dev(dx=0, dy=0, dz=0, core=c):
        return (lax.rem(z + dz, NZ) * 8 + lax.rem(y + dy, 4) * 2 + core, lax.rem(x + dx, 4))

    def rc(k, src, dst, to):
        return pltpu.make_async_remote_copy(
            src_ref=src, dst_ref=dst, send_sem=ssem.at[k], recv_sem=rsem.at[k],
            device_id=to, device_id_type=pl.DeviceIdType.MESH)

    loads = []
    for k in range(4):
        loads.append(pltpu.make_async_copy(tok.at[:, pl.ds(512 * k, 512)], tokv.at[k], lsem.at[k]))
        loads.append(pltpu.make_async_copy(wgt.at[:, pl.ds(384 * k, 384)], wfull.at[0, k], lsem.at[4 + k]))
    for ld in loads:
        ld.start()
    barrier = pltpu.get_barrier_semaphore()
    peers = [dev(dx=1), dev(dx=3), dev(dz=1), dev(dz=NZ - 1), dev(core=oc)]
    for dy in (1, 2, 3):
        peers += [dev(dy=dy), dev(dy=dy, core=oc)]
    for peer in peers:
        pl.semaphore_signal(barrier, inc=1, device_id=peer, device_id_type=pl.DeviceIdType.MESH)
    pl.semaphore_wait(barrier, len(peers))

    ya, za = lax.rem(y, 2), 2 + lax.rem(z, 2)
    aset = (ya, za)
    bset = (1 - ya, 5 - za)
    half = pl.ds(pl.multiple_of(256 * c, 256), 256)
    pend = []
    xd = {}
    for a in (0, 1):
        for slot, dx, k in ((3, 1, 0), (1, 3, 1)):
            src = wgt.at[half, pl.ds(pl.multiple_of(384 * aset[a], 128), 384)]
            cp = rc(X_DIR + 2 * a + k, src, wfull.at[slot, aset[a], half], dev(dx=dx))
            cp.start()
            xd[a, slot] = cp
            pend.append(cp)

    for ld in loads:
        ld.wait()

    def mm(slot, s, first=False):
        r = jnp.dot(tokv[lax.rem(x + slot, 4)], wfull[slot, s], preferred_element_type=F32)
        if first:
            acc[s] = r
        else:
            acc[s] += r

    for s in range(4):
        mm(0, s, True)

    cw, nb, xf = {}, {}, {}

    def core_send(role, slot, s):
        k = C_W + role * 3 + slot - 1
        cp = rc(k, wfull.at[slot, s, half], wfull.at[slot, s, half], dev(core=oc))
        cp.start()
        cw[role, slot] = cp
        pend.append(cp)

    step = 1 + 2 * c
    zstep = 1 + (NZ - 2) * c

    def side_send(a, slot):
        to = dev(dy=step) if a == 0 else dev(dz=zstep)
        k = (Y_W if a == 0 else Z_W) + slot - 1
        cp = rc(k, wfull.at[slot, aset[a], half], wfull.at[slot, aset[a], half], to)
        cp.start()
        nb[a, slot] = cp
        pend.append(cp)

    for a in (0, 1):
        for slot in (3, 1):
            xd[a, slot].wait_recv()
            row = 256 * c + (0 if slot == 3 else 128)
            part = pl.ds(pl.multiple_of(row, 128), 128)
            k = 0 if slot == 3 else 1
            cp = rc(X_FWD + 2 * a + k, wfull.at[slot, aset[a], part], wfull.at[2, aset[a], part],
                    dev(dx=1 if slot == 3 else 3))
            cp.start()
            xf[a, k] = cp
            pend.append(cp)
            side_send(a, slot)
            core_send(a, slot, aset[a])
    for a in (0, 1):
        for slot in (3, 1):
            cw[a, slot].wait_recv()
            mm(slot, aset[a])
    for slot in (3, 1):
        for a in (0, 1):
            nb[a, slot].wait_recv()
            core_send(2 + a, slot, bset[a])
    for a in (0, 1):
        xf[a, 0].wait_recv()
        xf[a, 1].wait_recv()
        side_send(a, 2)
        core_send(a, 2, aset[a])
    for slot in (3, 1):
        for a in (0, 1):
            cw[2 + a, slot].wait_recv()
            mm(slot, bset[a])
    for a in (0, 1):
        cw[a, 2].wait_recv()
        mm(2, aset[a])
    for a in (0, 1):
        nb[a, 2].wait_recv()
        core_send(2 + a, 2, bset[a])
    for a in (0, 1):
        cw[2 + a, 2].wait_recv()
        mm(2, bset[a])
    for j in range(12):
        proj[j] = acc[j // 3, :, (j % 3) * 128:(j % 3) * 128 + 128].astype(BF).reshape(8, 64, 128)

    def rows(j, b):
        return proj[j, pl.ds(2 * b, 2)].reshape(128, HD)

    def half_rows(j, b, which):
        return proj[j, 2 * b + which]

    def span(j, n, m):
        return proj[j, n // 64:m // 64].reshape(m - n, HD)

    fb = [lax.rem(foff[h], 4) for h in range(HEADS)]
    fc = [lax.div(foff[h], 4) for h in range(HEADS)]
    nbk = [noff[h] for h in range(HEADS)]
    for h in range(HEADS):
        fa_snd[h, 0:128] = rows(h, fb[h])
        fa_snd[h, 128:192] = half_rows(4 + h, fb[h], oc)
        fa_snd[h, 192:256] = half_rows(8 + h, fb[h], oc)
    fsib = rc(F_SIB, fa_snd, fa_rcv, dev(core=oc))
    fsib.start()
    pend.append(fsib)
    for h in range(HEADS):
        nqs[h] = rows(h, nbk[h])
        nks[h, 0] = rows(4 + h, nbk[h])
        nks[h, 1] = rows(8 + h, nbk[h])
    nin = []
    for j in (1, 2, 3):
        t = lax.rem(y + j, 4)
        for k, src, dst in ((N_Q, nqs.at[t], nq.at[y]), (N_KV, nks.at[t], nkv.at[c, :, y])):
            cp = rc(k + j - 1, src, dst, dev(dy=j))
            cp.start()
            nin.append(cp)
            pend.append(cp)
    nq[y] = nqs[y]
    nkv[c, 0, y] = nks[y, 0]
    nkv[c, 1, y] = nks[y, 1]

    qi = lax.broadcasted_iota(jnp.int32, (128, 128), 0)
    ki = lax.broadcasted_iota(jnp.int32, (128, 128), 1)
    causal = ki <= qi

    def local(h, i):
        n = 128 * i
        q = span(h, n, n + 128)
        s1 = jnp.where(causal, qk(q, span(4 + h, n, n + 128)), NEG)
        top = jnp.max(s1, axis=1, keepdims=True)
        if i:
            s0 = qk(q, span(4 + h, 0, n))
            top = jnp.maximum(top, jnp.max(s0, axis=1, keepdims=True))
        p1 = jnp.exp(s1 - top)
        tot = jnp.sum(p1, axis=1, keepdims=True)
        o = pv(p1, span(8 + h, n, n + 128))
        if i:
            p0 = jnp.exp(s0 - top)
            tot = tot + jnp.sum(p0, axis=1, keepdims=True)
            o = o + pv(p0, span(8 + h, 0, n))
        lo[h, i] = o / tot
        ll[h, i] = lanes(top + jnp.log(tot))

    for i in range(4):
        local(0, i)

    fsib.wait_recv()
    for h in range(HEADS):
        mine = jnp.full((128, HD), lax.rem(fc[h], 2), jnp.int32) == c

        def pick(own, other):
            return jnp.where(mine[0:own.shape[0]], own.astype(F32), other.astype(F32)).astype(BF)

        fsel[h, 0:128] = pick(rows(h, fb[h]), fa_rcv[h, 0:128])
        fsel[h, 128:192] = pick(half_rows(4 + h, fb[h], c), fa_rcv[h, 128:192])
        fsel[h, 192:256] = pick(half_rows(8 + h, fb[h], c), fa_rcv[h, 192:256])
    fin = []
    for j in (1, 2, 3):
        cp = rc(F_PLANE + j - 1, fsel.at[lax.rem(y + j, 4)], fcand.at[y], dev(dy=j))
        cp.start()
        fin.append(cp)
        pend.append(cp)
    fcand[y] = fsel[y]

    for cp in nin:
        cp.wait_recv()
    nsib = rc(N_SIB, nkv.at[c], nkv.at[c], dev(core=oc))
    nsib.start()
    pend.append(nsib)
    nup = rc(N_UP, nkv.at[c], ncross.at[c], dev(dz=1))
    odd = lax.rem(z, 2) == 1
    even = lax.rem(z, 2) == 0

    @pl.when(odd)
    def _():
        nup.start()

    for i in range(4):
        local(1, i)

    for cp in fin:
        cp.wait_recv()
    holder = lax.div(foff[y], 8)
    fq = fcand[holder, 0:128]
    kvf[0, 0] = fcand[holder, 128:192]
    kvf[0, 1] = fcand[holder, 192:256]

    ups, dns = {}, {}

    def send_up(t):
        ups[t] = rc(R_UP + t - 1, kvf.at[t - 1], kvf.at[t], dev(dz=1))
        ups[t].start()
        pend.append(ups[t])

    def send_dn(t):
        src = 0 if t == 1 else 17 - t
        dns[t] = rc(R_DN + t - 1, kvf.at[src], kvf.at[16 - t], dev(dz=NZ - 1))
        dns[t].start()
        pend.append(dns[t])

    send_up(1)
    send_dn(1)

    def ring(t):
        ups[t].wait_recv()
        if t < 8:
            send_up(t + 1)
        if t < 8:
            dns[t].wait_recv()
            if t < 7:
                send_dn(t + 1)

    for i in range(4):
        local(2, i)
    ring(1)
    for i in range(4):
        local(3, i)
    ring(2)

    nsib.wait_recv()

    def near_plane(i):
        q = nq[i]
        m = 128 * (i + 1)
        sa = qk(q, nkv[c, 0, 0:i + 1].reshape(m, HD))
        sb = qk(q, nkv[oc, 0, 0:i + 1].reshape(m, HD))
        kk = lax.broadcasted_iota(jnp.int32, (128, m), 1)
        qq = lax.broadcasted_iota(jnp.int32, (128, m), 0) + 128 * i
        sa = jnp.where(kk <= qq, sa, NEG)
        sb = jnp.where(kk < 128 * (i + c), sb, NEG)
        top = jnp.maximum(jnp.max(sa, axis=1, keepdims=True), jnp.max(sb, axis=1, keepdims=True))
        pa = jnp.exp(sa - top)
        pb = jnp.exp(sb - top)
        tot = jnp.sum(pa, axis=1, keepdims=True) + jnp.sum(pb, axis=1, keepdims=True)
        no[i] = pv(pa, nkv[c, 1, 0:i + 1].reshape(m, HD)) + pv(pb, nkv[oc, 1, 0:i + 1].reshape(m, HD))
        nm[i] = lanes(top)
        nl[i] = lanes(tot)

    nupsib = rc(N_UPSIB, ncross.at[c], ncross.at[c], dev(core=oc))

    @pl.when(even)
    def _():
        nup.wait_recv()
        nupsib.start()

    near_plane(0)
    near_plane(1)
    ring(3)
    near_plane(2)
    ring(4)
    near_plane(3)
    ring(5)

    @pl.when(even)
    def _():
        nupsib.wait_recv()

    def near_cross(i):
        q = nq[i]
        ss = [qk(q, ncross[d, 0].reshape(512, HD)) for d in (0, 1)]
        old = nm[i][:, 0:1]
        top = jnp.maximum(old, jnp.maximum(jnp.max(ss[0], axis=1, keepdims=True),
                                           jnp.max(ss[1], axis=1, keepdims=True)))
        w = jnp.exp(old - top)
        ps = [jnp.exp(s - top) for s in ss]
        tot = w * nl[i][:, 0:1] + jnp.sum(ps[0], axis=1, keepdims=True) + jnp.sum(ps[1], axis=1, keepdims=True)
        no[i] = w * no[i] + pv(ps[0], ncross[0, 1].reshape(512, HD)) + pv(ps[1], ncross[1, 1].reshape(512, HD))
        nm[i] = lanes(top)
        nl[i] = lanes(tot)

    cross = even & (z > 0)

    @pl.when(cross)
    def _():
        near_cross(0)
        near_cross(1)

    ring(6)

    @pl.when(cross)
    def _():
        near_cross(2)
        near_cross(3)

    ring(7)

    for i in range(4):
        nos[i] = (no[i] / nl[i]).astype(BF)
        nls[i] = (nm[i] + jnp.log(nl[i])).T[0:8]
    nback = []
    for j in (1, 2, 3):
        t = lax.rem(y + j, 4)
        for k, src, dst in ((N_O, nos.at[t], nor.at[y]), (N_L, nls.at[t], nlr.at[y])):
            cp = rc(k + j - 1, src, dst, dev(dy=j))
            cp.start()
            nback.append(cp)
            pend.append(cp)
    nor[y] = nos[y]
    nlr[y] = nls[y]

    ring(8)

    sf = qk(fq, kvf[:, 0].reshape(1024, HD))
    kk = lax.broadcasted_iota(jnp.int32, (128, 1024), 1)
    qq = lax.broadcasted_iota(jnp.int32, (128, 1024), 0)
    dist = lax.shift_right_logical(kk, 6)
    seen = (dist <= z) & ((dist > 0) | (kk + 64 * c <= qq))
    sf = jnp.where(seen, sf, NEG)
    top = jnp.max(sf, axis=1, keepdims=True)
    pf = jnp.exp(sf - top)
    tot = jnp.sum(pf, axis=1, keepdims=True)
    fos[...] = (pv(pf, kvf[:, 1].reshape(1024, HD)) / tot).astype(BF)
    fls[...] = lanes(top + jnp.log(tot)).T[0:8]
    fback = []
    n = 0
    for dy in (0, 1, 2, 3):
        for core in (c, oc):
            if dy == 0 and core is c:
                continue
            for k, src, dst in ((F_O, fos, fo.at[y, c]), (F_L, fls, fl.at[y, c])):
                cp = rc(k + n, src, dst, dev(dy=dy, core=core))
                cp.start()
                fback.append(cp)
                pend.append(cp)
            n += 1
    fo[y, c] = fos[...]
    fl[y, c] = fls[...]

    for cp in nback:
        cp.wait_recv()
    for cp in fback:
        cp.wait_recv()

    def spread(tile):
        return jnp.broadcast_to(tile[0:1], (128, 128)).T

    for h in range(HEADS):
        near_l = spread(nlr[h])
        far_l = [spread(fl[h, d]) for d in (0, 1)]
        near_o = nor[h].astype(F32)
        far_o = [fo[h, d].astype(F32) for d in (0, 1)]
        near_at = jnp.full((128, 128), nbk[h], jnp.int32)
        far_at = jnp.full((128, 128), foff[h], jnp.int32)
        for b in range(4):
            is_near = near_at == b
            is_far = far_at == lax.rem(seq, 8) * 4 + b
            ln = jnp.where(is_near, near_l, NEG)
            lf = [jnp.where(is_far, v, NEG) for v in far_l]
            l0 = ll[h, b]
            best = jnp.maximum(jnp.maximum(l0, ln), jnp.maximum(lf[0], lf[1]))
            w0 = jnp.exp(l0 - best)
            wn = jnp.exp(ln - best)
            wf = [jnp.exp(v - best) for v in lf]
            num = w0 * lo[h, b] + wn * near_o + wf[0] * far_o[0] + wf[1] * far_o[1]
            out[b * 128:b * 128 + 128, h * 128:h * 128 + 128] = (num / (w0 + wn + wf[0] + wf[1])).astype(BF)

    for cp in pend:
        cp.wait_send()

    @pl.when(odd)
    def _():
        nup.wait_send()

    @pl.when(even)
    def _():
        nupsib.wait_send()


def body(tokens, qkv_weight, near_offset, far_offset):
    vm = pltpu.VMEM
    mixed = pl.pallas_call(
        kernel,
        out_shape=jax.ShapeDtypeStruct((512, 512), BF),
        in_specs=[pl.BlockSpec(memory_space=pl.ANY)] * 2 + [pl.BlockSpec(memory_space=pltpu.SMEM)] * 2,
        out_specs=pl.BlockSpec(memory_space=pltpu.VMEM),
        scratch_shapes=[
            vm((4, 4, 512, 384), BF),
            vm((4, 512, 512), BF),
            vm((4, 512, 384), F32),
            vm((12, 8, 64, 128), BF),
            vm((4, 256, 128), BF),
            vm((4, 256, 128), BF),
            vm((4, 256, 128), BF),
            vm((4, 256, 128), BF),
            vm((16, 2, 64, 128), BF),
            vm((4, 128, 128), BF),
            vm((4, 2, 128, 128), BF),
            vm((4, 128, 128), BF),
            vm((2, 2, 4, 128, 128), BF),
            vm((2, 2, 4, 128, 128), BF),
            vm((4, 128, 128), F32),
            vm((4, 128, 128), F32),
            vm((4, 128, 128), F32),
            vm((4, 128, 128), BF),
            vm((4, 8, 128), F32),
            vm((4, 128, 128), BF),
            vm((4, 8, 128), F32),
            vm((128, 128), BF),
            vm((8, 128), F32),
            vm((4, 2, 128, 128), BF),
            vm((4, 2, 8, 128), F32),
            vm((4, 4, 128, 128), F32),
            vm((4, 4, 128, 128), F32),
            pltpu.SemaphoreType.DMA((N_SEM,)),
            pltpu.SemaphoreType.DMA((N_SEM,)),
            pltpu.SemaphoreType.DMA((8,)),
        ],
        compiler_params=pltpu.CompilerParams(
            collective_id=0, has_side_effects=True, vmem_limit_bytes=50 * 1024 * 1024),
    )(tokens[0], qkv_weight, near_offset, far_offset)
    return mixed[None]


def solution(mesh):
    in_specs = (P("fsdp", "seq", None), P("fsdp", None), P(), P())
    out_specs = P("fsdp", "seq", None)
    return jax.shard_map(body, mesh=mesh, in_specs=in_specs, out_specs=out_specs, check_vma=False)
```

time: 679 us -> 87.9 us (0.13)
  the two profiles are of different devices: /device:TPU:385 before, /device:TPU:1 now
where the time goes in v1:
time: 87.9 us; the launch traced here: 87.8 us
  Pallas kernels  84.3 us (96%)
  local copies, waits for them, and re-layouts  3.51 us (4%)
    pallas_call x1, Pallas kernels, body(): pl.pallas_call(kernel, out_shape=jax.ShapeDtypeStruct((512, 512), BF), in...  84.3 us
    unnamed x7, local copies, waits for them, and re-layouts  3.51 us

profile of v1, /device:TPU:1, one launch (start us, length us, event | category | flops | bytes accessed | tf_op | source)
XLA Modules:
  0.0 87.8 jit_solution(12708927781197117274)
XLA Ops:
  0.0 0.0 copy-start
  0.0 1.4 %copy-done = bf16[512,1536]{1,0:T(8,128)(2,1)S(1)} copy-done((bf16[512,1536]{1,0:T(8,128)(2,1)S(1)}, bf16[512,1536]{1,0:T(8,128)(2,1)}, u32[]{:S(2)}) %copy-start) | copy-done | bytes 1572888
  1.4 0.0 copy-start.1
  1.4 0.7 copy-done.1
  2.1 0.0 copy-start.2
  2.1 0.7 copy-done.2
  2.7 84.3 %shard_map.46 = bf16[512,512]{1,0:T(8,128)(2,1)S(1)} custom-call(bf16[512,2048]{1,0:T(8,128)(2,1)} %bitcast.3, bf16[512,1536]{1,0:T(8,128)(2,1)S(1)} %copy-done, s32[4]{0:T(128)S(1)} %copy-done.1, s32[4]{0:T(128)S(1)} %copy-done.2), custom_call_target="tpu_custom_call" | custom-call | tf_op jit(solution)/shard_map/pallas_call | solution.py:439
  87.0 0.8 copy.6
Async XLA Ops:
  0.0 1.4 %copy-start = (bf16[512,1536]{1,0:T(8,128)(2,1)S(1)}, bf16[512,1536]{1,0:T(8,128)(2,1)}, u32[]{:S(2)}) copy-start(bf16[512,1536]{1,0:T(8,128)(2,1)} %wgt.1) | copy-start | bytes 4718596
  1.4 0.7 copy-start.1
  2.1 0.7 copy-start.2

commit v2 on v1

v2 whole, which is shorter than its diff:
```python
import jax
import jax.numpy as jnp
from jax import lax
from jax.experimental import pallas as pl
from jax.experimental.pallas import tpu as pltpu
from jax.sharding import PartitionSpec as P

HEADS = 4
HD = 128
NZ = 16
SCALE = HD ** (-0.5)
NEG = -1e30
BF = jnp.bfloat16
F32 = jnp.float32

X_W, SIDE, SIDE_Q, C_X, C_SIDE, C_QX, C_QSIDE = 0, 12, 24, 30, 34, 46, 48
F_KV, F_Q, N_Q, N_KV, N_SIB, N_UP, N_UPSIB = 54, 61, 68, 71, 74, 75, 76
R_UP, R_DN, N_O, N_L, F_O, F_L = 77, 85, 92, 95, 98, 105
N_SEM = 112


def qk(q, k):
    return lax.dot_general(q, k, (((1,), (1,)), ((), ())), preferred_element_type=F32) * SCALE


def pv(p, v):
    return jnp.dot(p.astype(BF), v, preferred_element_type=F32)


def lanes(column):
    return jnp.broadcast_to(column, (128, 128))


def kernel(tok, wgt, noff_h, foff_h, out, wk, wv, wq, tokv, acc, proj, fkvs, fqs, fkvc, fqc, kvf,
           nqs, nks, nq, nkv, ncross, nm, nl, no, nos, nls, nor, nlr, fos, fls, fo, fl, lo, ll,
           noff, foff, ssem, rsem, lsem):
    seq = lax.axis_index("seq")
    x = lax.axis_index("fsdp")
    z = lax.div(seq, 8)
    y = lax.rem(lax.div(seq, 2), 4)
    c = lax.rem(seq, 2)
    oc = 1 - c

    def dev(dx=0, dy=0, dz=0, core=c):
        return (lax.rem(z + dz, NZ) * 8 + lax.rem(y + dy, 4) * 2 + core, lax.rem(x + dx, 4))

    pend = []

    def rc(k, src, dst, to):
        return pltpu.make_async_remote_copy(
            src_ref=src, dst_ref=dst, send_sem=ssem.at[k], recv_sem=rsem.at[k],
            device_id=to, device_id_type=pl.DeviceIdType.MESH)

    def go(k, src, dst, to):
        cp = rc(k, src, dst, to)
        cp.start()
        pend.append(cp)
        return cp

    loads = [pltpu.make_async_copy(tok.at[:, pl.ds(512 * k, 512)], tokv.at[k], lsem.at[k]) for k in range(4)]
    loads.append(pltpu.make_async_copy(wgt.at[:, pl.ds(512, 512)], wk.at[0], lsem.at[4]))
    loads.append(pltpu.make_async_copy(wgt.at[:, pl.ds(1024, 512)], wv.at[0], lsem.at[5]))
    for n in (0, 1):
        loads.append(pltpu.make_async_copy(wgt.at[:, pl.ds(256 * n, 256)], wq.at[0, n], lsem.at[6 + n]))
    loads.append(pltpu.make_async_copy(noff_h, noff, lsem.at[8]))
    loads.append(pltpu.make_async_copy(foff_h, foff, lsem.at[9]))
    for ld in loads:
        ld.start()
    barrier = pltpu.get_barrier_semaphore()
    peers = [dev(dx=d) for d in (1, 2, 3)] + [dev(dz=d) for d in (1, 2, NZ - 2, NZ - 1)] + [dev(core=oc)]
    for dy in (1, 2, 3):
        peers += [dev(dy=dy), dev(dy=dy, core=oc)]
    for peer in peers:
        pl.semaphore_signal(barrier, inc=1, device_id=peer, device_id_type=pl.DeviceIdType.MESH)
    pl.semaphore_wait(barrier, len(peers))

    place = (y, lax.rem(z, 4))

    def strip(pos, core=c):
        return pl.ds(pl.multiple_of(128 * pos + 64 * core, 64), 64)

    def q_cols(n):
        return pl.ds(256 * n, 256)

    kv_w = (wk, wv)
    xw, xq = {}, {}
    for slot, dx in ((1, 3), (2, 1), (3, 2)):
        for n in (0, 1):
            r = strip(place[n])
            xw[n, slot] = go(X_W + n * 3 + slot - 1, wgt.at[r, pl.ds(512 + 512 * n, 512)],
                             kv_w[n].at[slot, r], dev(dx=dx))
    for slot, dx in ((1, 3), (2, 1), (3, 2)):
        for n in (0, 1):
            r = strip(place[n])
            xq[n, slot] = go(X_W + 6 + n * 3 + slot - 1, wgt.at[r, q_cols(n)], wq.at[slot, n, r], dev(dx=dx))

    for ld in loads:
        ld.wait()

    def tk(slot):
        return tokv[lax.rem(x + (0, 1, 3, 2)[slot], 4)]

    def dot(a, b):
        return jnp.dot(a, b, preferred_element_type=F32)

    for n in (0, 1):
        acc[n] = dot(tk(0), kv_w[n][0])
        acc[2, :, 256 * n:256 * n + 256] = dot(tk(0), wq[0, n])

    def side_dev(n, j):
        if n == 0:
            return dev(dy=j)
        return dev(dz=(1, 2 + (NZ - 4) * c, NZ - 1)[j - 1])

    groups = (pl.ds(1, 2), pl.ds(3, 1))
    sw, cx, cs = {}, {}, {}
    for g in (0, 1):
        for n in (0, 1):
            for slot in ((1, 2), (3,))[g]:
                xw[n, slot].wait_recv()
            part = kv_w[n].at[groups[g], strip(place[n])]
            for j in (1, 2, 3):
                sw[g, n, j] = go(SIDE + g * 6 + n * 3 + j - 1, part, part, side_dev(n, j))
            cx[g, n] = go(C_X + g * 2 + n, part, part, dev(core=oc))

    def arrived(n, j):
        return strip(lax.rem(place[n] + 4 - j, 4))

    def side_arrivals(g):
        for j in (1, 3, 2):
            for n in (0, 1):
                sw[g, n, j].wait_recv()
                part = kv_w[n].at[groups[g], arrived(n, j)]
                cs[g, n, j] = go(C_SIDE + g * 6 + n * 3 + j - 1, part, part, dev(core=oc))

    side_arrivals(0)
    sq, cq = {}, {}
    rest = pl.ds(1, 3)
    for n in (0, 1):
        for slot in (1, 2, 3):
            xq[n, slot].wait_recv()
        part = wq.at[rest, n, strip(place[n])]
        for j in (1, 2, 3):
            sq[n, j] = go(SIDE_Q + n * 3 + j - 1, part, part, side_dev(n, j))
        cq[n, 0] = go(C_QX + n, part, part, dev(core=oc))
    for n in (0, 1):
        cx[0, n].wait_recv()
        for j in (1, 3, 2):
            cs[0, n, j].wait_recv()
        acc[n] += dot(tk(1), kv_w[n][1]) + dot(tk(2), kv_w[n][2])
    side_arrivals(1)
    for n in (0, 1):
        cx[1, n].wait_recv()
        for j in (1, 3, 2):
            cs[1, n, j].wait_recv()
        r = acc[n] + dot(tk(3), kv_w[n][3])
        for h in range(HEADS):
            proj[4 + 4 * n + h] = r[:, 128 * h:128 * h + 128].astype(BF).reshape(8, 64, HD)

    def rows(j, b):
        return proj[j, pl.ds(2 * b, 2)].reshape(128, HD)

    def span(j, n, m):
        return proj[j, n // 64:m // 64].reshape(m - n, HD)

    fb = [lax.rem(foff[h], 4) for h in range(HEADS)]
    nbk = [noff[h] for h in range(HEADS)]
    for h in range(HEADS):
        for d in (0, 1):
            fkvs[d, h, 0] = proj[4 + h, 2 * fb[h] + d]
            fkvs[d, h, 1] = proj[8 + h, 2 * fb[h] + d]
    me = 2 * y + c
    fin = []
    for j in (0, 1, 2, 3):
        t = lax.rem(y + j, 4)
        for core in (c, oc):
            if j or core is oc:
                fin.append(go(F_KV + len(fin), fkvs.at[core, t], fkvc.at[me], dev(dy=j, core=core)))
    fkvc[me] = fkvs[c, y]
    for h in range(HEADS):
        nks[h, 0] = rows(4 + h, nbk[h])
        nks[h, 1] = rows(8 + h, nbk[h])
    nin = []
    for j in (1, 3, 2):
        t = lax.rem(y + j, 4)
        nin.append(go(N_KV + j - 1, nks.at[t], nkv.at[c, :, y], dev(dy=j)))
    nkv[c, 0, y] = nks[y, 0]
    nkv[c, 1, y] = nks[y, 1]

    for j in (1, 3, 2):
        for n in (0, 1):
            sq[n, j].wait_recv()
            part = wq.at[rest, n, arrived(n, j)]
            cq[n, j] = go(C_QSIDE + n * 3 + j - 1, part, part, dev(core=oc))

    for cp in fin:
        cp.wait_recv()
    holder = lax.div(foff[y], 4)
    kvf[0] = fkvc[holder]
    ups, dns = {}, {}

    def send_up(d, hops):
        ups[d] = go(R_UP + d - 1, kvf.at[d - hops], kvf.at[d], dev(dz=hops))

    def send_dn(d, hops):
        src = 0 if d == hops else 16 - d + hops
        dns[d] = go(R_DN + d - 1, kvf.at[src], kvf.at[16 - d], dev(dz=NZ - hops))

    def ring(d):
        if d:
            ups[d].wait_recv()
        send_up(d + 2, 2)
        if d:
            dns[d].wait_recv()
        if d < 6:
            send_dn(d + 2, 2)
        send_up(d + 1, 1)
        send_dn(d + 1, 1)

    ring(0)
    for cp in nin:
        cp.wait_recv()
    nsib = go(N_SIB, nkv.at[c], nkv.at[c], dev(core=oc))
    nup = rc(N_UP, nkv.at[c], ncross.at[c], dev(dz=1))
    odd = lax.rem(z, 2) == 1
    even = lax.rem(z, 2) == 0

    @pl.when(odd)
    def _():
        nup.start()

    for n in (0, 1):
        for j in (0, 1, 3, 2):
            cq[n, j].wait_recv()
        r = acc[2, :, 256 * n:256 * n + 256]
        for slot in (1, 2, 3):
            r = r + dot(tk(slot), wq[slot, n])
        for h in (0, 1):
            proj[2 * n + h] = r[:, 128 * h:128 * h + 128].astype(BF).reshape(8, 64, HD)
    for h in range(HEADS):
        fqs[h] = rows(h, fb[h])
        nqs[h] = rows(h, nbk[h])
    qin = []
    for j in (1, 3, 2):
        t = lax.rem(y + j, 4)
        qin.append(go(N_Q + j - 1, nqs.at[t], nq.at[y], dev(dy=j)))
    nq[y] = nqs[y]
    fqin = []
    for j in (0, 1, 2, 3):
        t = lax.rem(y + j, 4)
        for core in (c, oc):
            if j or core is oc:
                fqin.append(go(F_Q + len(fqin), fqs.at[t], fqc.at[me], dev(dy=j, core=core)))
    fqc[me] = fqs[y]

    qi = lax.broadcasted_iota(jnp.int32, (128, 128), 0)
    ki = lax.broadcasted_iota(jnp.int32, (128, 128), 1)
    causal = ki <= qi

    def local(h, i):
        n = 128 * i
        q = span(h, n, n + 128)
        s1 = jnp.where(causal, qk(q, span(4 + h, n, n + 128)), NEG)
        top = jnp.max(s1, axis=1, keepdims=True)
        if i:
            s0 = qk(q, span(4 + h, 0, n))
            top = jnp.maximum(top, jnp.max(s0, axis=1, keepdims=True))
        p1 = jnp.exp(s1 - top)
        tot = jnp.sum(p1, axis=1, keepdims=True)
        o = pv(p1, span(8 + h, n, n + 128))
        if i:
            p0 = jnp.exp(s0 - top)
            tot = tot + jnp.sum(p0, axis=1, keepdims=True)
            o = o + pv(p0, span(8 + h, 0, n))
        lo[h, i] = o / tot
        ll[h, i] = lanes(top + jnp.log(tot))

    for i in range(4):
        local(0, i)
    ring(2)
    for i in range(4):
        local(1, i)

    nsib.wait_recv()

    def near_plane(i):
        q = nq[i]
        m = 128 * (i + 1)
        sa = qk(q, nkv[c, 0, 0:i + 1].reshape(m, HD))
        sb = qk(q, nkv[oc, 0, 0:i + 1].reshape(m, HD))
        kk = lax.broadcasted_iota(jnp.int32, (128, m), 1)
        qq = lax.broadcasted_iota(jnp.int32, (128, m), 0) + 128 * i
        sa = jnp.where(kk <= qq, sa, NEG)
        sb = jnp.where(kk < 128 * (i + c), sb, NEG)
        top = jnp.maximum(jnp.max(sa, axis=1, keepdims=True), jnp.max(sb, axis=1, keepdims=True))
        pa = jnp.exp(sa - top)
        pb = jnp.exp(sb - top)
        tot = jnp.sum(pa, axis=1, keepdims=True) + jnp.sum(pb, axis=1, keepdims=True)
        no[i] = pv(pa, nkv[c, 1, 0:i + 1].reshape(m, HD)) + pv(pb, nkv[oc, 1, 0:i + 1].reshape(m, HD))
        nm[i] = lanes(top)
        nl[i] = lanes(tot)

    nupsib = rc(N_UPSIB, ncross.at[c], ncross.at[c], dev(core=oc))

    @pl.when(even)
    def _():
        nup.wait_recv()
        nupsib.start()

    for cp in qin:
        cp.wait_recv()
    near_plane(0)
    near_plane(1)
    ring(4)
    near_plane(2)
    near_plane(3)
    for i in range(4):
        local(2, i)

    @pl.when(even)
    def _():
        nupsib.wait_recv()

    def near_cross(i):
        q = nq[i]
        ss = [qk(q, ncross[d, 0].reshape(512, HD)) for d in (0, 1)]
        old = nm[i][:, 0:1]
        top = jnp.maximum(old, jnp.maximum(jnp.max(ss[0], axis=1, keepdims=True),
                                           jnp.max(ss[1], axis=1, keepdims=True)))
        w = jnp.exp(old - top)
        ps = [jnp.exp(s - top) for s in ss]
        tot = w * nl[i][:, 0:1] + jnp.sum(ps[0], axis=1, keepdims=True) + jnp.sum(ps[1], axis=1, keepdims=True)
        no[i] = w * no[i] + pv(ps[0], ncross[0, 1].reshape(512, HD)) + pv(ps[1], ncross[1, 1].reshape(512, HD))
        nm[i] = lanes(top)
        nl[i] = lanes(tot)

    cross = even & (z > 0)

    @pl.when(cross)
    def _():
        for i in range(4):
            near_cross(i)

    for i in range(4):
        nos[i] = (no[i] / nl[i]).astype(BF)
        nls[i] = (nm[i] + jnp.log(nl[i])).T[0:8]
    nback = []
    for j in (1, 2, 3):
        t = lax.rem(y + j, 4)
        for k, src, dst in ((N_O, nos.at[t], nor.at[y]), (N_L, nls.at[t], nlr.at[y])):
            nback.append(go(k + j - 1, src, dst, dev(dy=j)))
    nor[y] = nos[y]
    nlr[y] = nls[y]

    ring(6)
    for i in range(4):
        local(3, i)
    for cp in fqin:
        cp.wait_recv()
    for d in (1, 3, 5, 7, 8):
        ups[d].wait_recv()
        if d < 8:
            dns[d].wait_recv()

    sf = qk(fqc[holder], kvf[:, 0].reshape(1024, HD))
    kk = lax.broadcasted_iota(jnp.int32, (128, 1024), 1)
    qq = lax.broadcasted_iota(jnp.int32, (128, 1024), 0)
    dist = lax.shift_right_logical(kk, 6)
    seen = (dist <= z) & ((dist > 0) | (kk + 64 * c <= qq))
    sf = jnp.where(seen, sf, NEG)
    top = jnp.max(sf, axis=1, keepdims=True)
    pf = jnp.exp(sf - top)
    tot = jnp.sum(pf, axis=1, keepdims=True)
    fos[...] = (pv(pf, kvf[:, 1].reshape(1024, HD)) / tot).astype(BF)
    fls[...] = lanes(top + jnp.log(tot)).T[0:8]
    fback = []
    n = 0
    for dy in (1, 3, 2, 0):
        for core in (c, oc):
            if dy == 0 and core is c:
                continue
            for k, src, dst in ((F_O, fos, fo.at[y, c]), (F_L, fls, fl.at[y, c])):
                fback.append(go(k + n, src, dst, dev(dy=dy, core=core)))
            n += 1
    fo[y, c] = fos[...]
    fl[y, c] = fls[...]

    for cp in nback:
        cp.wait_recv()
    for cp in fback:
        cp.wait_recv()

    def spread(tile):
        return jnp.broadcast_to(tile[0:1], (128, 128)).T

    for h in range(HEADS):
        near_l = spread(nlr[h])
        far_l = [spread(fl[h, d]) for d in (0, 1)]
        near_o = nor[h].astype(F32)
        far_o = [fo[h, d].astype(F32) for d in (0, 1)]
        near_at = jnp.full((128, 128), nbk[h], jnp.int32)
        far_at = jnp.full((128, 128), foff[h], jnp.int32)
        for b in range(4):
            is_near = near_at == b
            is_far = far_at == lax.rem(seq, 8) * 4 + b
            ln = jnp.where(is_near, near_l, NEG)
            lf = [jnp.where(is_far, v, NEG) for v in far_l]
            l0 = ll[h, b]
            best = jnp.maximum(jnp.maximum(l0, ln), jnp.maximum(lf[0], lf[1]))
            w0 = jnp.exp(l0 - best)
            wn = jnp.exp(ln - best)
            wf = [jnp.exp(v - best) for v in lf]
            num = w0 * lo[h, b] + wn * near_o + wf[0] * far_o[0] + wf[1] * far_o[1]
            out[b * 128:b * 128 + 128, h * 128:h * 128 + 128] = (num / (w0 + wn + wf[0] + wf[1])).astype(BF)

    for cp in pend:
        cp.wait_send()

    @pl.when(odd)
    def _():
        nup.wait_send()

    @pl.when(even)
    def _():
        nupsib.wait_send()


def body(tokens, qkv_weight, near_offset, far_offset):
    vm = pltpu.VMEM
    mixed = pl.pallas_call(
        kernel,
        out_shape=jax.ShapeDtypeStruct((512, 512), BF),
        in_specs=[pl.BlockSpec(memory_space=pl.ANY)] * 4,
        out_specs=pl.BlockSpec(memory_space=pltpu.VMEM),
        scratch_shapes=[
            vm((4, 512, 512), BF),
            vm((4, 512, 512), BF),
            vm((4, 2, 512, 256), BF),
            vm((4, 512, 512), BF),
            vm((3, 512, 512), F32),
            vm((12, 8, 64, 128), BF),
            vm((2, 4, 2, 64, 128), BF),
            vm((4, 128, 128), BF),
            vm((8, 2, 64, 128), BF),
            vm((8, 128, 128), BF),
            vm((16, 2, 64, 128), BF),
            vm((4, 128, 128), BF),
            vm((4, 2, 128, 128), BF),
            vm((4, 128, 128), BF),
            vm((2, 2, 4, 128, 128), BF),
            vm((2, 2, 4, 128, 128), BF),
            vm((4, 128, 128), F32),
            vm((4, 128, 128), F32),
            vm((4, 128, 128), F32),
            vm((4, 128, 128), BF),
            vm((4, 8, 128), F32),
            vm((4, 128, 128), BF),
            vm((4, 8, 128), F32),
            vm((128, 128), BF),
            vm((8, 128), F32),
            vm((4, 2, 128, 128), BF),
            vm((4, 2, 8, 128), F32),
            vm((4, 4, 128, 128), F32),
            vm((4, 4, 128, 128), F32),
            pltpu.SMEM((4,), jnp.int32),
            pltpu.SMEM((4,), jnp.int32),
            pltpu.SemaphoreType.DMA((N_SEM,)),
            pltpu.SemaphoreType.DMA((N_SEM,)),
            pltpu.SemaphoreType.DMA((10,)),
        ],
        compiler_params=pltpu.CompilerParams(
            collective_id=0, has_side_effects=True, vmem_limit_bytes=60 * 1024 * 1024),
    )(tokens[0], qkv_weight, near_offset, far_offset)
    return mixed[None]


def solution(mesh):
    in_specs = (P("fsdp", "seq", None), P("fsdp", None), P(), P())
    out_specs = P("fsdp", "seq", None)
    return jax.shard_map(body, mesh=mesh, in_specs=in_specs, out_specs=out_specs, check_vma=False)
```

time: 87.9 us -> 72.8 us (0.83)
  Pallas kernels: 84.3 us -> 70.7 us
  local copies, waits for them, and re-layouts: 3.51 us -> 1.87 us
    pallas_call x1, Pallas kernels: 84.3 us -> 70.7 us  [body(): pl.pallas_call(kernel, out_shape=jax.ShapeDtypeStruct((512, 512), BF), in...]
    unnamed x7 -> x1, local copies, waits for them, and re-layouts: 3.51 us -> 1.87 us
where the time goes in v2:
time: 72.8 us; the launch traced here: 72.6 us
  Pallas kernels  70.7 us (97%)
  local copies, waits for them, and re-layouts  1.87 us (3%)
    pallas_call x1, Pallas kernels, body(): pl.pallas_call(kernel, out_shape=jax.ShapeDtypeStruct((512, 512), BF), in...  70.7 us
    unnamed x1, local copies, waits for them, and re-layouts  1.87 us

profile of v2, /device:TPU:1, one launch (start us, length us, event | category | flops | bytes accessed | tf_op | source)
XLA Modules:
  0.0 72.6 jit_solution(4509842026508877603)
XLA Ops:
  0.0 70.7 %shard_map.46 = bf16[512,512]{1,0:T(8,128)(2,1)} custom-call(bf16[512,2048]{1,0:T(8,128)(2,1)} %bitcast.2, bf16[512,1536]{1,0:T(8,128)(2,1)} %wgt.1, s32[4]{0:T(128)} %noff_h.1, s32[4]{0:T(128)} %foff_h.1), custom_call_target="tpu_custom_call" | custom-call | tf_op jit(solution)/shard_map/pallas_call | solution.py:430
  70.8 1.9 %copy.6 = bf16[1,512,512]{2,1,0:T(8,128)(2,1)} copy(bf16[1,512,512]{2,1,0:T(8,128)(2,1)} %bitcast.3) | data formatting | bytes 1048576

commit v3 on v2

--- a/solution.py
+++ b/solution.py
@@ -32,7 +32,7 @@
 
 
 def kernel(tok, wgt, noff_h, foff_h, out, wk, wv, wq, tokv, acc, proj, fkvs, fqs, fkvc, fqc, kvf,
-           nqs, nks, nq, nkv, ncross, nm, nl, no, nos, nls, nor, nlr, fos, fls, fo, fl, lo, ll,
+           nqs, nks, nq, nkv, ncross, nm, nl, no, nos, nls, nor, nlr, fos, fls, fo, fl, lo, ll, nw,
            noff, foff, ssem, rsem, lsem):
     seq = lax.axis_index("seq")
     x = lax.axis_index("fsdp")
@@ -133,7 +133,6 @@
                 part = kv_w[n].at[groups[g], arrived(n, j)]
                 cs[g, n, j] = go(C_SIDE + g * 6 + n * 3 + j - 1, part, part, dev(core=oc))
 
-    side_arrivals(0)
     sq, cq = {}, {}
     rest = pl.ds(1, 3)
     for n in (0, 1):
@@ -143,6 +142,7 @@
         for j in (1, 2, 3):
             sq[n, j] = go(SIDE_Q + n * 3 + j - 1, part, part, side_dev(n, j))
         cq[n, 0] = go(C_QX + n, part, part, dev(core=oc))
+    side_arrivals(0)
     for n in (0, 1):
         cx[0, n].wait_recv()
         for j in (1, 3, 2):
@@ -275,11 +275,14 @@
         lo[h, i] = o / tot
         ll[h, i] = lanes(top + jnp.log(tot))
 
-    for i in range(4):
-        local(0, i)
     ring(2)
-    for i in range(4):
-        local(1, i)
+    for h in (0, 1):
+        for i in range(4):
+            local(h, i)
+    ring(4)
+    for h in (2, 3):
+        for i in range(4):
+            local(h, i)
 
     nsib.wait_recv()
 
@@ -300,6 +303,11 @@
         nm[i] = lanes(top)
         nl[i] = lanes(tot)
 
+    for cp in qin:
+        cp.wait_recv()
+    near_plane(0)
+    near_plane(1)
+    ring(6)
     nupsib = rc(N_UPSIB, ncross.at[c], ncross.at[c], dev(core=oc))
 
     @pl.when(even)
@@ -307,15 +315,8 @@
         nup.wait_recv()
         nupsib.start()
 
-    for cp in qin:
-        cp.wait_recv()
-    near_plane(0)
-    near_plane(1)
-    ring(4)
     near_plane(2)
     near_plane(3)
-    for i in range(4):
-        local(2, i)
 
     @pl.when(even)
     def _():
@@ -352,9 +353,6 @@
     nor[y] = nos[y]
     nlr[y] = nls[y]
 
-    ring(6)
-    for i in range(4):
-        local(3, i)
     for cp in fqin:
         cp.wait_recv()
     for d in (1, 3, 5, 7, 8):
@@ -385,33 +383,39 @@
     fo[y, c] = fos[...]
     fl[y, c] = fls[...]
 
-    for cp in nback:
-        cp.wait_recv()
-    for cp in fback:
-        cp.wait_recv()
-
     def spread(tile):
         return jnp.broadcast_to(tile[0:1], (128, 128)).T
 
+    for cp in nback:
+        cp.wait_recv()
     for h in range(HEADS):
         near_l = spread(nlr[h])
+        near_o = nor[h].astype(F32)
+        near_at = jnp.full((128, 128), nbk[h], jnp.int32)
+        for b in range(4):
+            ln = jnp.where(near_at == b, near_l, NEG)
+            l0 = ll[h, b]
+            best = jnp.maximum(l0, ln)
+            w0 = jnp.exp(l0 - best)
+            wn = jnp.exp(ln - best)
+            lo[h, b] = w0 * lo[h, b] + wn * near_o
+            nw[h, b] = w0 + wn
+            ll[h, b] = best
+    for cp in fback:
+        cp.wait_recv()
+    for h in range(HEADS):
         far_l = [spread(fl[h, d]) for d in (0, 1)]
-        near_o = nor[h].astype(F32)
         far_o = [fo[h, d].astype(F32) for d in (0, 1)]
-        near_at = jnp.full((128, 128), nbk[h], jnp.int32)
         far_at = jnp.full((128, 128), foff[h], jnp.int32)
         for b in range(4):
-            is_near = near_at == b
             is_far = far_at == lax.rem(seq, 8) * 4 + b
-            ln = jnp.where(is_near, near_l, NEG)
             lf = [jnp.where(is_far, v, NEG) for v in far_l]
             l0 = ll[h, b]
-            best = jnp.maximum(jnp.maximum(l0, ln), jnp.maximum(lf[0], lf[1]))
+            best = jnp.maximum(l0, jnp.maximum(lf[0], lf[1]))
             w0 = jnp.exp(l0 - best)
-            wn = jnp.exp(ln - best)
             wf = [jnp.exp(v - best) for v in lf]
-            num = w0 * lo[h, b] + wn * near_o + wf[0] * far_o[0] + wf[1] * far_o[1]
-            out[b * 128:b * 128 + 128, h * 128:h * 128 + 128] = (num / (w0 + wn + wf[0] + wf[1])).astype(BF)
+            num = w0 * lo[h, b] + wf[0] * far_o[0] + wf[1] * far_o[1]
+            out[b * 128:b * 128 + 128, h * 128:h * 128 + 128] = (num / (w0 * nw[h, b] + wf[0] + wf[1])).astype(BF)
 
     for cp in pend:
         cp.wait_send()
@@ -462,6 +466,7 @@
             vm((4, 2, 8, 128), F32),
             vm((4, 4, 128, 128), F32),
             vm((4, 4, 128, 128), F32),
+            vm((4, 4, 128, 128), F32),
             pltpu.SMEM((4,), jnp.int32),
             pltpu.SMEM((4,), jnp.int32),
             pltpu.SemaphoreType.DMA((N_SEM,)),

time: 72.8 us -> 72.9 us (level)
  no operation moved by 1% of the time
where the time goes in v3:
time: 72.9 us; the launch traced here: 72.7 us
  Pallas kernels  70.9 us (97%)
  local copies, waits for them, and re-layouts  1.87 us (3%)
    pallas_call x1, Pallas kernels, body(): pl.pallas_call(kernel, out_shape=jax.ShapeDtypeStruct((512, 512), BF), in...  70.9 us
    unnamed x1, local copies, waits for them, and re-layouts  1.87 us

profile of v3, /device:TPU:1, one launch (start us, length us, event | category | flops | bytes accessed | tf_op | source)
XLA Modules:
  0.0 72.7 jit_solution(121995369041060915)
XLA Ops:
  0.0 70.9 %shard_map.46 = bf16[512,512]{1,0:T(8,128)(2,1)} custom-call(bf16[512,2048]{1,0:T(8,128)(2,1)} %bitcast.2, bf16[512,1536]{1,0:T(8,128)(2,1)} %wgt.1, s32[4]{0:T(128)} %noff_h.1, s32[4]{0:T(128)} %foff_h.1), custom_call_target="tpu_custom_call" | custom-call | tf_op jit(solution)/shard_map/pallas_call | solution.py:434
  70.9 1.9 %copy.6 = bf16[1,512,512]{2,1,0:T(8,128)(2,1)} copy(bf16[1,512,512]{2,1,0:T(8,128)(2,1)} %bitcast.3) | data formatting | bytes 1048576

commit v4 on v3

--- a/solution.py
+++ b/solution.py
@@ -13,10 +13,10 @@
 BF = jnp.bfloat16
 F32 = jnp.float32
 
-X_W, SIDE, SIDE_Q, C_X, C_SIDE, C_QX, C_QSIDE = 0, 12, 24, 30, 34, 46, 48
-F_KV, F_Q, N_Q, N_KV, N_SIB, N_UP, N_UPSIB = 54, 61, 68, 71, 74, 75, 76
-R_UP, R_DN, N_O, N_L, F_O, F_L = 77, 85, 92, 95, 98, 105
-N_SEM = 112
+X_W, X_Q, SIDE, C_X, C_SIDE, C_Q = 0, 6, 9, 21, 25, 37
+F_KV, F_Q, N_Q, N_KV, N_SIB, N_UP, N_UPSIB = 40, 47, 54, 57, 60, 61, 62
+R_UP, R_DN, N_O, F_O = 63, 71, 78, 81
+N_SEM = 88
 
 
 def qk(q, k):
@@ -32,7 +32,7 @@
 
 
 def kernel(tok, wgt, noff_h, foff_h, out, wk, wv, wq, tokv, acc, proj, fkvs, fqs, fkvc, fqc, kvf,
-           nqs, nks, nq, nkv, ncross, nm, nl, no, nos, nls, nor, nlr, fos, fls, fo, fl, lo, ll, nw,
+           nqs, nks, nq, nkv, ncross, nm, nl, no, nos, nor, fos, fo, lo, ll, nw,
            noff, foff, ssem, rsem, lsem):
     seq = lax.axis_index("seq")
     x = lax.axis_index("fsdp")
@@ -60,10 +60,9 @@
     loads = [pltpu.make_async_copy(tok.at[:, pl.ds(512 * k, 512)], tokv.at[k], lsem.at[k]) for k in range(4)]
     loads.append(pltpu.make_async_copy(wgt.at[:, pl.ds(512, 512)], wk.at[0], lsem.at[4]))
     loads.append(pltpu.make_async_copy(wgt.at[:, pl.ds(1024, 512)], wv.at[0], lsem.at[5]))
-    for n in (0, 1):
-        loads.append(pltpu.make_async_copy(wgt.at[:, pl.ds(256 * n, 256)], wq.at[0, n], lsem.at[6 + n]))
-    loads.append(pltpu.make_async_copy(noff_h, noff, lsem.at[8]))
-    loads.append(pltpu.make_async_copy(foff_h, foff, lsem.at[9]))
+    loads.append(pltpu.make_async_copy(wgt.at[:, pl.ds(0, 512)], wq.at[0], lsem.at[6]))
+    loads.append(pltpu.make_async_copy(noff_h, noff, lsem.at[7]))
+    loads.append(pltpu.make_async_copy(foff_h, foff, lsem.at[8]))
     for ld in loads:
         ld.start()
     barrier = pltpu.get_barrier_semaphore()
@@ -79,9 +78,6 @@
     def strip(pos, core=c):
         return pl.ds(pl.multiple_of(128 * pos + 64 * core, 64), 64)
 
-    def q_cols(n):
-        return pl.ds(256 * n, 256)
-
     kv_w = (wk, wv)
     xw, xq = {}, {}
     for slot, dx in ((1, 3), (2, 1), (3, 2)):
@@ -89,10 +85,9 @@
             r = strip(place[n])
             xw[n, slot] = go(X_W + n * 3 + slot - 1, wgt.at[r, pl.ds(512 + 512 * n, 512)],
                              kv_w[n].at[slot, r], dev(dx=dx))
+    half = pl.ds(pl.multiple_of(256 * c, 256), 256)
     for slot, dx in ((1, 3), (2, 1), (3, 2)):
-        for n in (0, 1):
-            r = strip(place[n])
-            xq[n, slot] = go(X_W + 6 + n * 3 + slot - 1, wgt.at[r, q_cols(n)], wq.at[slot, n, r], dev(dx=dx))
+        xq[slot] = go(X_Q + slot - 1, wgt.at[half, pl.ds(0, 512)], wq.at[slot, half], dev(dx=dx))
 
     for ld in loads:
         ld.wait()
@@ -105,7 +100,7 @@
 
     for n in (0, 1):
         acc[n] = dot(tk(0), kv_w[n][0])
-        acc[2, :, 256 * n:256 * n + 256] = dot(tk(0), wq[0, n])
+    acc[2] = dot(tk(0), wq[0])
 
     def side_dev(n, j):
         if n == 0:
@@ -133,15 +128,6 @@
                 part = kv_w[n].at[groups[g], arrived(n, j)]
                 cs[g, n, j] = go(C_SIDE + g * 6 + n * 3 + j - 1, part, part, dev(core=oc))
 
-    sq, cq = {}, {}
-    rest = pl.ds(1, 3)
-    for n in (0, 1):
-        for slot in (1, 2, 3):
-            xq[n, slot].wait_recv()
-        part = wq.at[rest, n, strip(place[n])]
-        for j in (1, 2, 3):
-            sq[n, j] = go(SIDE_Q + n * 3 + j - 1, part, part, side_dev(n, j))
-        cq[n, 0] = go(C_QX + n, part, part, dev(core=oc))
     side_arrivals(0)
     for n in (0, 1):
         cx[0, n].wait_recv()
@@ -187,11 +173,10 @@
     nkv[c, 0, y] = nks[y, 0]
     nkv[c, 1, y] = nks[y, 1]
 
-    for j in (1, 3, 2):
-        for n in (0, 1):
-            sq[n, j].wait_recv()
-            part = wq.at[rest, n, arrived(n, j)]
-            cq[n, j] = go(C_QSIDE + n * 3 + j - 1, part, part, dev(core=oc))
+    cq = {}
+    for slot in (1, 2, 3):
+        xq[slot].wait_recv()
+        cq[slot] = go(C_Q + slot - 1, wq.at[slot, half], wq.at[slot, half], dev(core=oc))
 
     for cp in fin:
         cp.wait_recv()
@@ -229,14 +214,12 @@
     def _():
         nup.start()
 
-    for n in (0, 1):
-        for j in (0, 1, 3, 2):
-            cq[n, j].wait_recv()
-        r = acc[2, :, 256 * n:256 * n + 256]
-        for slot in (1, 2, 3):
-            r = r + dot(tk(slot), wq[slot, n])
-        for h in (0, 1):
-            proj[2 * n + h] = r[:, 128 * h:128 * h + 128].astype(BF).reshape(8, 64, HD)
+    for slot in (1, 2, 3):
+        cq[slot].wait_recv()
+    r = acc[2] + dot(tk(1), wq[1]) + dot(tk(2), wq[2]) + dot(tk(3), wq[3])
+    for h in range(HEADS):
+        proj[h] = r[:, 128 * h:128 * h + 128].astype(BF).reshape(8, 64, HD)
+    ring(2)
     for h in range(HEADS):
         fqs[h] = rows(h, fb[h])
         nqs[h] = rows(h, nbk[h])
@@ -252,6 +235,13 @@
             if j or core is oc:
                 fqin.append(go(F_Q + len(fqin), fqs.at[t], fqc.at[me], dev(dy=j, core=core)))
     fqc[me] = fqs[y]
+
+    def pack(lse):
+        t = lse.T[0:16]
+        a = t.astype(BF).astype(F32)
+        b = (t - a).astype(BF).astype(F32)
+        row = lax.broadcasted_iota(jnp.int32, (16, 128), 0)
+        return jnp.where(row == 0, a, jnp.where(row == 1, b, t - a - b)).astype(BF)
 
     qi = lax.broadcasted_iota(jnp.int32, (128, 128), 0)
     ki = lax.broadcasted_iota(jnp.int32, (128, 128), 1)
@@ -275,7 +265,6 @@
         lo[h, i] = o / tot
         ll[h, i] = lanes(top + jnp.log(tot))
 
-    ring(2)
     for h in (0, 1):
         for i in range(4):
             local(h, i)
@@ -343,15 +332,13 @@
             near_cross(i)
 
     for i in range(4):
-        nos[i] = (no[i] / nl[i]).astype(BF)
-        nls[i] = (nm[i] + jnp.log(nl[i])).T[0:8]
+        nos[i, 0:128] = (no[i] / nl[i]).astype(BF)
+        nos[i, 128:144] = pack(nm[i] + jnp.log(nl[i]))
     nback = []
     for j in (1, 2, 3):
         t = lax.rem(y + j, 4)
-        for k, src, dst in ((N_O, nos.at[t], nor.at[y]), (N_L, nls.at[t], nlr.at[y])):
-            nback.append(go(k + j - 1, src, dst, dev(dy=j)))
+        nback.append(go(N_O + j - 1, nos.at[t], nor.at[y], dev(dy=j)))
     nor[y] = nos[y]
-    nlr[y] = nls[y]
 
     for cp in fqin:
         cp.wait_recv()
@@ -369,28 +356,27 @@
     top = jnp.max(sf, axis=1, keepdims=True)
     pf = jnp.exp(sf - top)
     tot = jnp.sum(pf, axis=1, keepdims=True)
-    fos[...] = (pv(pf, kvf[:, 1].reshape(1024, HD)) / tot).astype(BF)
-    fls[...] = lanes(top + jnp.log(tot)).T[0:8]
+    fos[0:128] = (pv(pf, kvf[:, 1].reshape(1024, HD)) / tot).astype(BF)
+    fos[128:144] = pack(lanes(top + jnp.log(tot)))
     fback = []
     n = 0
     for dy in (1, 3, 2, 0):
         for core in (c, oc):
             if dy == 0 and core is c:
                 continue
-            for k, src, dst in ((F_O, fos, fo.at[y, c]), (F_L, fls, fl.at[y, c])):
-                fback.append(go(k + n, src, dst, dev(dy=dy, core=core)))
+            fback.append(go(F_O + n, fos, fo.at[y, c], dev(dy=dy, core=core)))
             n += 1
     fo[y, c] = fos[...]
-    fl[y, c] = fls[...]
 
     def spread(tile):
-        return jnp.broadcast_to(tile[0:1], (128, 128)).T
+        t = tile.astype(F32)
+        return jnp.broadcast_to(t[0:1] + t[1:2] + t[2:3], (128, 128)).T
 
     for cp in nback:
         cp.wait_recv()
     for h in range(HEADS):
-        near_l = spread(nlr[h])
-        near_o = nor[h].astype(F32)
+        near_l = spread(nor[h, 128:144])
+        near_o = nor[h, 0:128].astype(F32)
         near_at = jnp.full((128, 128), nbk[h], jnp.int32)
         for b in range(4):
             ln = jnp.where(near_at == b, near_l, NEG)
@@ -404,8 +390,8 @@
     for cp in fback:
         cp.wait_recv()
     for h in range(HEADS):
-        far_l = [spread(fl[h, d]) for d in (0, 1)]
-        far_o = [fo[h, d].astype(F32) for d in (0, 1)]
+        far_l = [spread(fo[h, d, 128:144]) for d in (0, 1)]
+        far_o = [fo[h, d, 0:128].astype(F32) for d in (0, 1)]
         far_at = jnp.full((128, 128), foff[h], jnp.int32)
         for b in range(4):
             is_far = far_at == lax.rem(seq, 8) * 4 + b
@@ -439,7 +425,7 @@
         scratch_shapes=[
             vm((4, 512, 512), BF),
             vm((4, 512, 512), BF),
-            vm((4, 2, 512, 256), BF),
+            vm((4, 512, 512), BF),
             vm((4, 512, 512), BF),
             vm((3, 512, 512), F32),
             vm((12, 8, 64, 128), BF),
@@ -456,14 +442,10 @@
             vm((4, 128, 128), F32),
             vm((4, 128, 128), F32),
             vm((4, 128, 128), F32),
-            vm((4, 128, 128), BF),
-            vm((4, 8, 128), F32),
-            vm((4, 128, 128), BF),
-            vm((4, 8, 128), F32),
-            vm((128, 128), BF),
-            vm((8, 128), F32),
-            vm((4, 2, 128, 128), BF),
-            vm((4, 2, 8, 128), F32),
+            vm((4, 144, 128), BF),
+            vm((4, 144, 128), BF),
+            vm((144, 128), BF),
+            vm((4, 2, 144, 128), BF),
             vm((4, 4, 128, 128), F32),
             vm((4, 4, 128, 128), F32),
             vm((4, 4, 128, 128), F32),
@@ -471,7 +453,7 @@
             pltpu.SMEM((4,), jnp.int32),
             pltpu.SemaphoreType.DMA((N_SEM,)),
             pltpu.SemaphoreType.DMA((N_SEM,)),
-            pltpu.SemaphoreType.DMA((10,)),
+            pltpu.SemaphoreType.DMA((9,)),
         ],
         compiler_params=pltpu.CompilerParams(
             collective_id=0, has_side_effects=True, vmem_limit_bytes=60 * 1024 * 1024),

time: 72.9 us -> 71.5 us (0.981)
  Pallas kernels: 70.9 us -> 69.5 us
    pallas_call x1, Pallas kernels: 70.9 us -> 69.5 us  [body(): pl.pallas_call(kernel, out_shape=jax.ShapeDtypeStruct((512, 512), BF), in...]
where the time goes in v4:
time: 71.5 us; the launch traced here: 71.4 us
  Pallas kernels  69.5 us (97%)
  local copies, waits for them, and re-layouts  1.87 us (3%)
    pallas_call x1, Pallas kernels, body(): pl.pallas_call(kernel, out_shape=jax.ShapeDtypeStruct((512, 512), BF), in...  69.5 us
    unnamed x1, local copies, waits for them, and re-layouts  1.87 us

profile of v4, /device:TPU:1, one launch (start us, length us, event | category | flops | bytes accessed | tf_op | source)
XLA Modules:
  0.0 71.4 jit_solution(16666282115644618450)
XLA Ops:
  0.0 69.5 %shard_map.46 = bf16[512,512]{1,0:T(8,128)(2,1)} custom-call(bf16[512,2048]{1,0:T(8,128)(2,1)} %bitcast.2, bf16[512,1536]{1,0:T(8,128)(2,1)} %wgt.1, s32[4]{0:T(128)} %noff_h.1, s32[4]{0:T(128)} %foff_h.1), custom_call_target="tpu_custom_call" | custom-call | tf_op jit(solution)/shard_map/pallas_call | solution.py:420
  69.5 1.9 %copy.6 = bf16[1,512,512]{2,1,0:T(8,128)(2,1)} copy(bf16[1,512,512]{2,1,0:T(8,128)(2,1)} %bitcast.3) | data formatting | bytes 1048576

commit v5 on v4

--- a/solution.py
+++ b/solution.py
@@ -66,7 +66,7 @@
     for ld in loads:
         ld.start()
     barrier = pltpu.get_barrier_semaphore()
-    peers = [dev(dx=d) for d in (1, 2, 3)] + [dev(dz=d) for d in (1, 2, NZ - 2, NZ - 1)] + [dev(core=oc)]
+    peers = [dev(dx=d) for d in (1, 2, 3)] + [dev(dz=d) for d in (1, 2, 3, 6, NZ - 6, NZ - 3, NZ - 2, NZ - 1)] + [dev(core=oc)]
     for dy in (1, 2, 3):
         peers += [dev(dy=dy), dev(dy=dy, core=oc)]
     for peer in peers:
@@ -163,6 +163,38 @@
             if j or core is oc:
                 fin.append(go(F_KV + len(fin), fkvs.at[core, t], fkvc.at[me], dev(dy=j, core=core)))
     fkvc[me] = fkvs[c, y]
+
+    cq = {}
+    for slot in (1, 2, 3):
+        xq[slot].wait_recv()
+        cq[slot] = go(C_Q + slot - 1, wq.at[slot, half], wq.at[slot, half], dev(core=oc))
+
+    for cp in fin:
+        cp.wait_recv()
+    holder = lax.div(foff[y], 4)
+    kvf[0] = fkvc[holder]
+    ups, dns = {}, {}
+
+    def send_up(d, hops):
+        ups[d] = go(R_UP + d - 1, kvf.at[d - hops], kvf.at[d], dev(dz=hops))
+
+    def send_dn(d, hops):
+        src = 0 if d == hops else 16 - d + hops
+        dns[d] = go(R_DN + d - 1, kvf.at[src], kvf.at[16 - d], dev(dz=NZ - hops))
+
+    for d in (6, 3, 2, 1):
+        send_up(d, d)
+        send_dn(d, d)
+
+    def relay(d):
+        ups[d].wait_recv()
+        send_up(d + 2, 2)
+        dns[d].wait_recv()
+        if d == 3:
+            send_dn(d + 2, 2)
+        send_up(d + 1, 1)
+        send_dn(d + 1, 1)
+
     for h in range(HEADS):
         nks[h, 0] = rows(4 + h, nbk[h])
         nks[h, 1] = rows(8 + h, nbk[h])
@@ -173,53 +205,11 @@
     nkv[c, 0, y] = nks[y, 0]
     nkv[c, 1, y] = nks[y, 1]
 
-    cq = {}
-    for slot in (1, 2, 3):
-        xq[slot].wait_recv()
-        cq[slot] = go(C_Q + slot - 1, wq.at[slot, half], wq.at[slot, half], dev(core=oc))
-
-    for cp in fin:
-        cp.wait_recv()
-    holder = lax.div(foff[y], 4)
-    kvf[0] = fkvc[holder]
-    ups, dns = {}, {}
-
-    def send_up(d, hops):
-        ups[d] = go(R_UP + d - 1, kvf.at[d - hops], kvf.at[d], dev(dz=hops))
-
-    def send_dn(d, hops):
-        src = 0 if d == hops else 16 - d + hops
-        dns[d] = go(R_DN + d - 1, kvf.at[src], kvf.at[16 - d], dev(dz=NZ - hops))
-
-    def ring(d):
-        if d:
-            ups[d].wait_recv()
-        send_up(d + 2, 2)
-        if d:
-            dns[d].wait_recv()
-        if d < 6:
-            send_dn(d + 2, 2)
-        send_up(d + 1, 1)
-        send_dn(d + 1, 1)
-
-    ring(0)
-    for cp in nin:
-        cp.wait_recv()
-    nsib = go(N_SIB, nkv.at[c], nkv.at[c], dev(core=oc))
-    nup = rc(N_UP, nkv.at[c], ncross.at[c], dev(dz=1))
-    odd = lax.rem(z, 2) == 1
-    even = lax.rem(z, 2) == 0
-
-    @pl.when(odd)
-    def _():
-        nup.start()
-
     for slot in (1, 2, 3):
         cq[slot].wait_recv()
     r = acc[2] + dot(tk(1), wq[1]) + dot(tk(2), wq[2]) + dot(tk(3), wq[3])
     for h in range(HEADS):
         proj[h] = r[:, 128 * h:128 * h + 128].astype(BF).reshape(8, 64, HD)
-    ring(2)
     for h in range(HEADS):
         fqs[h] = rows(h, fb[h])
         nqs[h] = rows(h, nbk[h])
@@ -235,6 +225,18 @@
             if j or core is oc:
                 fqin.append(go(F_Q + len(fqin), fqs.at[t], fqc.at[me], dev(dy=j, core=core)))
     fqc[me] = fqs[y]
+    relay(3)
+    for cp in nin:
+        cp.wait_recv()
+    nsib = go(N_SIB, nkv.at[c], nkv.at[c], dev(core=oc))
+    nup = rc(N_UP, nkv.at[c], ncross.at[c], dev(dz=1))
+    odd = lax.rem(z, 2) == 1
+    even = lax.rem(z, 2) == 0
+
+    @pl.when(odd)
+    def _():
+        nup.start()
+    relay(6)
 
     def pack(lse):
         t = lse.T[0:16]
@@ -265,13 +267,19 @@
         lo[h, i] = o / tot
         ll[h, i] = lanes(top + jnp.log(tot))
 
-    for h in (0, 1):
+    for h in (0, 1, 2):
         for i in range(4):
             local(h, i)
-    ring(4)
-    for h in (2, 3):
-        for i in range(4):
-            local(h, i)
+
+    nupsib = rc(N_UPSIB, ncross.at[c], ncross.at[c], dev(core=oc))
+
+    @pl.when(even)
+    def _():
+        nup.wait_recv()
+        nupsib.start()
+
+    for i in range(4):
+        local(3, i)
 
     nsib.wait_recv()
 
@@ -296,14 +304,6 @@
         cp.wait_recv()
     near_plane(0)
     near_plane(1)
-    ring(6)
-    nupsib = rc(N_UPSIB, ncross.at[c], ncross.at[c], dev(core=oc))
-
-    @pl.when(even)
-    def _():
-        nup.wait_recv()
-        nupsib.start()
-
     near_plane(2)
     near_plane(3)
 
@@ -342,7 +342,7 @@
 
     for cp in fqin:
         cp.wait_recv()
-    for d in (1, 3, 5, 7, 8):
+    for d in (1, 2, 4, 5, 7, 8):
         ups[d].wait_recv()
         if d < 8:
             dns[d].wait_recv()

time: 71.5 us -> 75.5 us (1.056)
  Pallas kernels: 69.5 us -> 73.5 us
    pallas_call x1, Pallas kernels: 69.5 us -> 73.5 us  [body(): pl.pallas_call(kernel, out_shape=jax.ShapeDtypeStruct((512, 512), BF), in...]
where the time goes in v5:
time: 75.5 us; the launch traced here: 75.4 us
  Pallas kernels  73.5 us (97%)
  local copies, waits for them, and re-layouts  1.87 us (2%)
    pallas_call x1, Pallas kernels, body(): pl.pallas_call(kernel, out_shape=jax.ShapeDtypeStruct((512, 512), BF), in...  73.5 us
    unnamed x1, local copies, waits for them, and re-layouts  1.87 us

profile of v5, /device:TPU:1, one launch (start us, length us, event | category | flops | bytes accessed | tf_op | source)
XLA Modules:
  0.0 75.4 jit_solution(566882909740394669)
XLA Ops:
  0.0 73.5 %shard_map.46 = bf16[512,512]{1,0:T(8,128)(2,1)} custom-call(bf16[512,2048]{1,0:T(8,128)(2,1)} %bitcast.2, bf16[512,1536]{1,0:T(8,128)(2,1)} %wgt.1, s32[4]{0:T(128)} %noff_h.1, s32[4]{0:T(128)} %foff_h.1), custom_call_target="tpu_custom_call" | custom-call | tf_op jit(solution)/shard_map/pallas_call | solution.py:420
  73.5 1.9 %copy.6 = bf16[1,512,512]{2,1,0:T(8,128)(2,1)} copy(bf16[1,512,512]{2,1,0:T(8,128)(2,1)} %bitcast.3) | data formatting | bytes 1048576

commit v6 on v4

--- a/solution.py
+++ b/solution.py
@@ -14,9 +14,9 @@
 F32 = jnp.float32
 
 X_W, X_Q, SIDE, C_X, C_SIDE, C_Q = 0, 6, 9, 21, 25, 37
-F_KV, F_Q, N_Q, N_KV, N_SIB, N_UP, N_UPSIB = 40, 47, 54, 57, 60, 61, 62
-R_UP, R_DN, N_O, F_O = 63, 71, 78, 81
-N_SEM = 88
+F_KV, F_Q, N_Q, N_KV, N_SIB = 40, 47, 54, 57, 60
+R_UP, R_DN, N_O, F_O, N_QD, N_OC = 61, 69, 76, 79, 86, 90
+N_SEM = 94
 
 
 def qk(q, k):
@@ -32,7 +32,7 @@
 
 
 def kernel(tok, wgt, noff_h, foff_h, out, wk, wv, wq, tokv, acc, proj, fkvs, fqs, fkvc, fqc, kvf,
-           nqs, nks, nq, nkv, ncross, nm, nl, no, nos, nor, fos, fo, lo, ll, nw,
+           nqs, nks, nq, nkv, ncq, cos, cor, nos, nor, fos, fo, lo, ll, nw,
            noff, foff, ssem, rsem, lsem):
     seq = lax.axis_index("seq")
     x = lax.axis_index("fsdp")
@@ -68,7 +68,7 @@
     barrier = pltpu.get_barrier_semaphore()
     peers = [dev(dx=d) for d in (1, 2, 3)] + [dev(dz=d) for d in (1, 2, NZ - 2, NZ - 1)] + [dev(core=oc)]
     for dy in (1, 2, 3):
-        peers += [dev(dy=dy), dev(dy=dy, core=oc)]
+        peers += [dev(dy=dy), dev(dy=dy, core=oc), dev(dy=dy, dz=1), dev(dy=dy, dz=NZ - 1)]
     for peer in peers:
         pl.semaphore_signal(barrier, inc=1, device_id=peer, device_id_type=pl.DeviceIdType.MESH)
     pl.semaphore_wait(barrier, len(peers))
@@ -206,13 +206,9 @@
     for cp in nin:
         cp.wait_recv()
     nsib = go(N_SIB, nkv.at[c], nkv.at[c], dev(core=oc))
-    nup = rc(N_UP, nkv.at[c], ncross.at[c], dev(dz=1))
     odd = lax.rem(z, 2) == 1
-    even = lax.rem(z, 2) == 0
-
-    @pl.when(odd)
-    def _():
-        nup.start()
+    upper = jnp.logical_not(odd) & (z > 0)
+    lower = odd & (z < NZ - 1)
 
     for slot in (1, 2, 3):
         cq[slot].wait_recv()
@@ -223,6 +219,13 @@
     for h in range(HEADS):
         fqs[h] = rows(h, fb[h])
         nqs[h] = rows(h, nbk[h])
+    down = [rc(N_QD + j, nqs.at[lax.rem(y + j, 4)], ncq.at[y], dev(dy=j, dz=NZ - 1)) for j in (0, 1, 2, 3)]
+
+    @pl.when(upper)
+    def _():
+        for j in (0, 1, 3, 2):
+            down[j].start()
+
     qin = []
     for j in (1, 3, 2):
         t = lax.rem(y + j, 4)
@@ -269,11 +272,18 @@
         for i in range(4):
             local(h, i)
     ring(4)
-    for h in (2, 3):
-        for i in range(4):
-            local(h, i)
-
-    nsib.wait_recv()
+
+    def finish(to, i, pairs, tops):
+        top = tops[0]
+        for t in tops[1:]:
+            top = jnp.maximum(top, t)
+        tot, o = 0.0, 0.0
+        for sc, v in pairs:
+            p = jnp.exp(sc - top)
+            tot = tot + jnp.sum(p, axis=1, keepdims=True)
+            o = o + pv(p, v)
+        to[i, 0:128] = (o / tot).astype(BF)
+        to[i, 128:144] = pack(lanes(top + jnp.log(tot)))
 
     def near_plane(i):
         q = nq[i]
@@ -284,62 +294,43 @@
         qq = lax.broadcasted_iota(jnp.int32, (128, m), 0) + 128 * i
         sa = jnp.where(kk <= qq, sa, NEG)
         sb = jnp.where(kk < 128 * (i + c), sb, NEG)
-        top = jnp.maximum(jnp.max(sa, axis=1, keepdims=True), jnp.max(sb, axis=1, keepdims=True))
-        pa = jnp.exp(sa - top)
-        pb = jnp.exp(sb - top)
-        tot = jnp.sum(pa, axis=1, keepdims=True) + jnp.sum(pb, axis=1, keepdims=True)
-        no[i] = pv(pa, nkv[c, 1, 0:i + 1].reshape(m, HD)) + pv(pb, nkv[oc, 1, 0:i + 1].reshape(m, HD))
-        nm[i] = lanes(top)
-        nl[i] = lanes(tot)
-
+        finish(nos, i, [(sa, nkv[c, 1, 0:i + 1].reshape(m, HD)), (sb, nkv[oc, 1, 0:i + 1].reshape(m, HD))],
+               [jnp.max(sa, axis=1, keepdims=True), jnp.max(sb, axis=1, keepdims=True)])
+
+    nsib.wait_recv()
     for cp in qin:
         cp.wait_recv()
-    near_plane(0)
-    near_plane(1)
+    for i in range(4):
+        near_plane(i)
+    nback = []
+    for j in (1, 3, 2):
+        nback.append(go(N_O + j - 1, nos.at[lax.rem(y + j, 4)], nor.at[y], dev(dy=j)))
+    nor[y] = nos[y]
+
+    back = [rc(N_OC + j, cos.at[lax.rem(y + j, 4)], cor.at[y], dev(dy=j, dz=1)) for j in (0, 1, 2, 3)]
+
+    @pl.when(lower)
+    def _():
+        for j in (0, 1, 3, 2):
+            down[j].wait_recv()
+        for i in range(4):
+            q = ncq[i]
+            ss = [qk(q, nkv[d, 0].reshape(512, HD)) for d in (0, 1)]
+            finish(cos, i, [(ss[d], nkv[d, 1].reshape(512, HD)) for d in (0, 1)],
+                   [jnp.max(t, axis=1, keepdims=True) for t in ss])
+        for j in (0, 1, 3, 2):
+            back[j].start()
+
+    @pl.when(jnp.logical_not(upper))
+    def _():
+        for h in range(HEADS):
+            cor[h, 0:128] = jnp.zeros((128, HD), BF)
+            cor[h, 128:144] = jnp.full((16, HD), NEG, BF)
+
     ring(6)
-    nupsib = rc(N_UPSIB, ncross.at[c], ncross.at[c], dev(core=oc))
-
-    @pl.when(even)
-    def _():
-        nup.wait_recv()
-        nupsib.start()
-
-    near_plane(2)
-    near_plane(3)
-
-    @pl.when(even)
-    def _():
-        nupsib.wait_recv()
-
-    def near_cross(i):
-        q = nq[i]
-        ss = [qk(q, ncross[d, 0].reshape(512, HD)) for d in (0, 1)]
-        old = nm[i][:, 0:1]
-        top = jnp.maximum(old, jnp.maximum(jnp.max(ss[0], axis=1, keepdims=True),
-                                           jnp.max(ss[1], axis=1, keepdims=True)))
-        w = jnp.exp(old - top)
-        ps = [jnp.exp(s - top) for s in ss]
-        tot = w * nl[i][:, 0:1] + jnp.sum(ps[0], axis=1, keepdims=True) + jnp.sum(ps[1], axis=1, keepdims=True)
-        no[i] = w * no[i] + pv(ps[0], ncross[0, 1].reshape(512, HD)) + pv(ps[1], ncross[1, 1].reshape(512, HD))
-        nm[i] = lanes(top)
-        nl[i] = lanes(tot)
-
-    cross = even & (z > 0)
-
-    @pl.when(cross)
-    def _():
+    for h in (2, 3):
         for i in range(4):
-            near_cross(i)
-
-    for i in range(4):
-        nos[i, 0:128] = (no[i] / nl[i]).astype(BF)
-        nos[i, 128:144] = pack(nm[i] + jnp.log(nl[i]))
-    nback = []
-    for j in (1, 2, 3):
-        t = lax.rem(y + j, 4)
-        nback.append(go(N_O + j - 1, nos.at[t], nor.at[y], dev(dy=j)))
-    nor[y] = nos[y]
-
+            local(h, i)
     for cp in fqin:
         cp.wait_recv()
     for d in (1, 3, 5, 7, 8):
@@ -374,9 +365,20 @@
 
     for cp in nback:
         cp.wait_recv()
-    for h in range(HEADS):
-        near_l = spread(nor[h, 128:144])
-        near_o = nor[h, 0:128].astype(F32)
+
+    @pl.when(upper)
+    def _():
+        for j in (0, 1, 3, 2):
+            back[j].wait_recv()
+
+    for h in range(HEADS):
+        plane_l = spread(nor[h, 128:144])
+        cross_l = spread(cor[h, 128:144])
+        near_l = jnp.maximum(plane_l, cross_l)
+        wp = jnp.exp(plane_l - near_l)
+        wc = jnp.exp(cross_l - near_l)
+        near_o = wp * nor[h, 0:128].astype(F32) + wc * cor[h, 0:128].astype(F32)
+        near_w = wp + wc
         near_at = jnp.full((128, 128), nbk[h], jnp.int32)
         for b in range(4):
             ln = jnp.where(near_at == b, near_l, NEG)
@@ -385,7 +387,7 @@
             w0 = jnp.exp(l0 - best)
             wn = jnp.exp(ln - best)
             lo[h, b] = w0 * lo[h, b] + wn * near_o
-            nw[h, b] = w0 + wn
+            nw[h, b] = w0 + wn * near_w
             ll[h, b] = best
     for cp in fback:
         cp.wait_recv()
@@ -406,13 +408,15 @@
     for cp in pend:
         cp.wait_send()
 
-    @pl.when(odd)
-    def _():
-        nup.wait_send()
-
-    @pl.when(even)
-    def _():
-        nupsib.wait_send()
+    @pl.when(upper)
+    def _():
+        for cp in down:
+            cp.wait_send()
+
+    @pl.when(lower)
+    def _():
+        for cp in back:
+            cp.wait_send()
 
 
 def body(tokens, qkv_weight, near_offset, far_offset):
@@ -438,10 +442,9 @@
             vm((4, 2, 128, 128), BF),
             vm((4, 128, 128), BF),
             vm((2, 2, 4, 128, 128), BF),
-            vm((2, 2, 4, 128, 128), BF),
-            vm((4, 128, 128), F32),
-            vm((4, 128, 128), F32),
-            vm((4, 128, 128), F32),
+            vm((4, 128, 128), BF),
+            vm((4, 144, 128), BF),
+            vm((4, 144, 128), BF),
             vm((4, 144, 128), BF),
             vm((4, 144, 128), BF),
             vm((144, 128), BF),

time: 71.5 us -> 68.6 us (0.959)
  Pallas kernels: 69.5 us -> 66.6 us
    pallas_call x1, Pallas kernels: 69.5 us -> 66.6 us  [body(): pl.pallas_call(kernel, out_shape=jax.ShapeDtypeStruct((512, 512), BF), in...]
where the time goes in v6:
time: 68.6 us; the launch traced here: 68.5 us
  Pallas kernels  66.6 us (97%)
  local copies, waits for them, and re-layouts  1.87 us (3%)
    pallas_call x1, Pallas kernels, body(): pl.pallas_call(kernel, out_shape=jax.ShapeDtypeStruct((512, 512), BF), in...  66.6 us
    unnamed x1, local copies, waits for them, and re-layouts  1.87 us

profile of v6, /device:TPU:1, one launch (start us, length us, event | category | flops | bytes accessed | tf_op | source)
XLA Modules:
  0.0 68.5 jit_solution(10190819235152501624)
XLA Ops:
  0.0 66.6 %shard_map.46 = bf16[512,512]{1,0:T(8,128)(2,1)} custom-call(bf16[512,2048]{1,0:T(8,128)(2,1)} %bitcast.2, bf16[512,1536]{1,0:T(8,128)(2,1)} %wgt.1, s32[4]{0:T(128)} %noff_h.1, s32[4]{0:T(128)} %foff_h.1), custom_call_target="tpu_custom_call" | custom-call | tf_op jit(solution)/shard_map/pallas_call | solution.py:424
  66.6 1.9 %copy.6 = bf16[1,512,512]{2,1,0:T(8,128)(2,1)} copy(bf16[1,512,512]{2,1,0:T(8,128)(2,1)} %bitcast.3) | data formatting | bytes 1048576

commit v7 on v6

--- a/solution.py
+++ b/solution.py
@@ -80,15 +80,15 @@
 
     kv_w = (wk, wv)
     xw, xq = {}, {}
-    for slot, dx in ((1, 3), (2, 1), (3, 2)):
+
+    def x_send(slot, dx):
         for n in (0, 1):
             r = strip(place[n])
             xw[n, slot] = go(X_W + n * 3 + slot - 1, wgt.at[r, pl.ds(512 + 512 * n, 512)],
                              kv_w[n].at[slot, r], dev(dx=dx))
-    half = pl.ds(pl.multiple_of(256 * c, 256), 256)
-    for slot, dx in ((1, 3), (2, 1), (3, 2)):
-        xq[slot] = go(X_Q + slot - 1, wgt.at[half, pl.ds(0, 512)], wq.at[slot, half], dev(dx=dx))
-
+
+    x_send(1, 3)
+    x_send(2, 1)
     for ld in loads:
         ld.wait()
 
@@ -100,7 +100,7 @@
 
     for n in (0, 1):
         acc[n] = dot(tk(0), kv_w[n][0])
-    acc[2] = dot(tk(0), wq[0])
+    x_send(3, 2)
 
     def side_dev(n, j):
         if n == 0:
@@ -118,6 +118,10 @@
                 sw[g, n, j] = go(SIDE + g * 6 + n * 3 + j - 1, part, part, side_dev(n, j))
             cx[g, n] = go(C_X + g * 2 + n, part, part, dev(core=oc))
 
+    half = pl.ds(pl.multiple_of(256 * c, 256), 256)
+    for slot, dx in ((1, 3), (2, 1), (3, 2)):
+        xq[slot] = go(X_Q + slot - 1, wgt.at[half, pl.ds(0, 512)], wq.at[slot, half], dev(dx=dx))
+
     def arrived(n, j):
         return strip(lax.rem(place[n] + 4 - j, 4))
 
@@ -128,13 +132,14 @@
                 part = kv_w[n].at[groups[g], arrived(n, j)]
                 cs[g, n, j] = go(C_SIDE + g * 6 + n * 3 + j - 1, part, part, dev(core=oc))
 
+    acc[2] = dot(tk(0), wq[0])
     side_arrivals(0)
+    side_arrivals(1)
     for n in (0, 1):
         cx[0, n].wait_recv()
         for j in (1, 3, 2):
             cs[0, n, j].wait_recv()
         acc[n] += dot(tk(1), kv_w[n][1]) + dot(tk(2), kv_w[n][2])
-    side_arrivals(1)
     for n in (0, 1):
         cx[1, n].wait_recv()
         for j in (1, 3, 2):
@@ -333,29 +338,45 @@
             local(h, i)
     for cp in fqin:
         cp.wait_recv()
-    for d in (1, 3, 5, 7, 8):
+    for d in (1, 3, 5):
         ups[d].wait_recv()
-        if d < 8:
-            dns[d].wait_recv()
-
-    sf = qk(fqc[holder], kvf[:, 0].reshape(1024, HD))
-    kk = lax.broadcasted_iota(jnp.int32, (128, 1024), 1)
-    qq = lax.broadcasted_iota(jnp.int32, (128, 1024), 0)
-    dist = lax.shift_right_logical(kk, 6)
-    seen = (dist <= z) & ((dist > 0) | (kk + 64 * c <= qq))
-    sf = jnp.where(seen, sf, NEG)
-    top = jnp.max(sf, axis=1, keepdims=True)
-    pf = jnp.exp(sf - top)
-    tot = jnp.sum(pf, axis=1, keepdims=True)
-    fos[0:128] = (pv(pf, kvf[:, 1].reshape(1024, HD)) / tot).astype(BF)
+        dns[d].wait_recv()
+
+    fq = fqc[holder]
+    ranges = ((0, 7), (10, 16), (7, 10))
+
+    def far_scores(a, b):
+        m = 64 * (b - a)
+        kk = lax.broadcasted_iota(jnp.int32, (128, m), 1) + 64 * a
+        qq = lax.broadcasted_iota(jnp.int32, (128, m), 0)
+        seen = lax.shift_right_logical(kk, 6) <= z
+        if a == 0:
+            seen = seen & ((kk >= 64) | (kk + 64 * c <= qq))
+        return jnp.where(seen, qk(fq, kvf[a:b, 0].reshape(m, HD)), NEG)
+
+    def far_part(top, a, b, sc):
+        p = jnp.exp(sc - top)
+        return jnp.sum(p, axis=1, keepdims=True), pv(p, kvf[a:b, 1].reshape(64 * (b - a), HD))
+
+    early = [far_scores(a, b) for a, b in ranges[:2]]
+    top0 = jnp.maximum(jnp.max(early[0], axis=1, keepdims=True), jnp.max(early[1], axis=1, keepdims=True))
+    parts = [far_part(top0, a, b, sc) for (a, b), sc in zip(ranges[:2], early)]
+    for cp in (ups[7], dns[7], ups[8]):
+        cp.wait_recv()
+    late = far_scores(*ranges[2])
+    top = jnp.maximum(top0, jnp.max(late, axis=1, keepdims=True))
+    w = jnp.exp(top0 - top)
+    tl, ol = far_part(top, *ranges[2], late)
+    tot = w * (parts[0][0] + parts[1][0]) + tl
+    fos[0:128] = ((w * (parts[0][1] + parts[1][1]) + ol) / tot).astype(BF)
     fos[128:144] = pack(lanes(top + jnp.log(tot)))
-    fback = []
+    fback = [[], [], [], []]
     n = 0
-    for dy in (1, 3, 2, 0):
+    for dy in (2, 1, 3, 0):
         for core in (c, oc):
             if dy == 0 and core is c:
                 continue
-            fback.append(go(F_O + n, fos, fo.at[y, c], dev(dy=dy, core=core)))
+            fback[dy].append(go(F_O + n, fos, fo.at[y, c], dev(dy=dy, core=core)))
             n += 1
     fo[y, c] = fos[...]
 
@@ -389,9 +410,10 @@
             lo[h, b] = w0 * lo[h, b] + wn * near_o
             nw[h, b] = w0 + wn * near_w
             ll[h, b] = best
-    for cp in fback:
-        cp.wait_recv()
-    for h in range(HEADS):
+    for dy in (0, 1, 3, 2):
+        for cp in fback[dy]:
+            cp.wait_recv()
+        h = lax.rem(y + 4 - dy, 4)
         far_l = [spread(fo[h, d, 128:144]) for d in (0, 1)]
         far_o = [fo[h, d, 0:128].astype(F32) for d in (0, 1)]
         far_at = jnp.full((128, 128), foff[h], jnp.int32)
@@ -403,7 +425,8 @@
             w0 = jnp.exp(l0 - best)
             wf = [jnp.exp(v - best) for v in lf]
             num = w0 * lo[h, b] + wf[0] * far_o[0] + wf[1] * far_o[1]
-            out[b * 128:b * 128 + 128, h * 128:h * 128 + 128] = (num / (w0 * nw[h, b] + wf[0] + wf[1])).astype(BF)
+            out[b * 128:b * 128 + 128, pl.ds(pl.multiple_of(h * 128, 128), 128)] = (
+                num / (w0 * nw[h, b] + wf[0] + wf[1])).astype(BF)
 
     for cp in pend:
         cp.wait_send()

time: 68.6 us -> 65.9 us (0.961)
  Pallas kernels: 66.6 us -> 63.2 us
    pallas_call x1, Pallas kernels: 66.6 us -> 63.2 us  [body(): pl.pallas_call(kernel, out_shape=jax.ShapeDtypeStruct((512, 512), BF), in...]
where the time goes in v7:
time: 65.9 us; the launch traced here: 65.1 us
  Pallas kernels  63.2 us (96%)
  local copies, waits for them, and re-layouts  1.87 us (3%)
    pallas_call x1, Pallas kernels, body(): pl.pallas_call(kernel, out_shape=jax.ShapeDtypeStruct((512, 512), BF), in...  63.2 us
    unnamed x1, local copies, waits for them, and re-layouts  1.87 us

profile of v7, /device:TPU:1, one launch (start us, length us, event | category | flops | bytes accessed | tf_op | source)
XLA Modules:
  0.0 65.1 jit_solution(6070564831375313490)
XLA Ops:
  0.0 63.2 %shard_map.46 = bf16[512,512]{1,0:T(8,128)(2,1)} custom-call(bf16[512,2048]{1,0:T(8,128)(2,1)} %bitcast.2, bf16[512,1536]{1,0:T(8,128)(2,1)} %wgt.1, s32[4]{0:T(128)} %noff_h.1, s32[4]{0:T(128)} %foff_h.1), custom_call_target="tpu_custom_call" | custom-call | tf_op jit(solution)/shard_map/pallas_call | solution.py:447
  63.2 1.9 %copy.6 = bf16[1,512,512]{2,1,0:T(8,128)(2,1)} copy(bf16[1,512,512]{2,1,0:T(8,128)(2,1)} %bitcast.3) | data formatting | bytes 1048576

commit v8 on v7

--- a/solution.py
+++ b/solution.py
@@ -65,6 +65,7 @@
     loads.append(pltpu.make_async_copy(foff_h, foff, lsem.at[8]))
     for ld in loads:
         ld.start()
+    kvf[...] = jnp.zeros_like(kvf)
     barrier = pltpu.get_barrier_semaphore()
     peers = [dev(dx=d) for d in (1, 2, 3)] + [dev(dz=d) for d in (1, 2, NZ - 2, NZ - 1)] + [dev(core=oc)]
     for dy in (1, 2, 3):
@@ -187,21 +188,44 @@
         cp.wait_recv()
     holder = lax.div(foff[y], 4)
     kvf[0] = fkvc[holder]
-    ups, dns = {}, {}
+    ups, dns, maybe = {}, {}, []
+
+    def start_if(cp, needed):
+        maybe.append((cp, needed))
+
+        @pl.when(needed)
+        def _():
+            cp.start()
 
     def send_up(d, hops):
-        ups[d] = go(R_UP + d - 1, kvf.at[d - hops], kvf.at[d], dev(dz=hops))
+        ups[d] = rc(R_UP + d - 1, kvf.at[d - hops], kvf.at[d], dev(dz=hops))
+        start_if(ups[d], (z + hops < NZ) & (z + hops >= d))
+
+    def wanted_dn(place_z, d):
+        late = place_z + d >= NZ
+        return late if d % 2 else late | (place_z + d <= 6)
 
     def send_dn(d, hops):
         src = 0 if d == hops else 16 - d + hops
-        dns[d] = go(R_DN + d - 1, kvf.at[src], kvf.at[16 - d], dev(dz=NZ - hops))
+        dns[d] = rc(R_DN + d - 1, kvf.at[src], kvf.at[16 - d], dev(dz=NZ - hops))
+        start_if(dns[d], wanted_dn(lax.rem(z + NZ - hops, NZ), d))
+
+    def got_up(d):
+        @pl.when(z >= d)
+        def _():
+            ups[d].wait_recv()
+
+    def got_dn(d):
+        @pl.when(wanted_dn(z, d))
+        def _():
+            dns[d].wait_recv()
 
     def ring(d):
         if d:
-            ups[d].wait_recv()
+            got_up(d)
         send_up(d + 2, 2)
         if d:
-            dns[d].wait_recv()
+            got_dn(d)
         if d < 6:
             send_dn(d + 2, 2)
         send_up(d + 1, 1)
@@ -339,8 +363,8 @@
     for cp in fqin:
         cp.wait_recv()
     for d in (1, 3, 5):
-        ups[d].wait_recv()
-        dns[d].wait_recv()
+        got_up(d)
+        got_dn(d)
 
     fq = fqc[holder]
     ranges = ((0, 7), (10, 16), (7, 10))
@@ -361,8 +385,9 @@
     early = [far_scores(a, b) for a, b in ranges[:2]]
     top0 = jnp.maximum(jnp.max(early[0], axis=1, keepdims=True), jnp.max(early[1], axis=1, keepdims=True))
     parts = [far_part(top0, a, b, sc) for (a, b), sc in zip(ranges[:2], early)]
-    for cp in (ups[7], dns[7], ups[8]):
-        cp.wait_recv()
+    got_up(7)
+    got_dn(7)
+    got_up(8)
     late = far_scores(*ranges[2])
     top = jnp.maximum(top0, jnp.max(late, axis=1, keepdims=True))
     w = jnp.exp(top0 - top)
@@ -430,6 +455,8 @@
 
     for cp in pend:
         cp.wait_send()
+    for cp, needed in maybe:
+        pl.when(needed)(cp.wait_send)
 
     @pl.when(upper)
     def _():

time: 65.9 us -> 63.1 us (0.958); the launches traced: 65.1 us -> 63 us
  Pallas kernels: 63.2 us -> 61.1 us
    pallas_call x1, Pallas kernels: 63.2 us -> 61.1 us  [body(): pl.pallas_call(kernel, out_shape=jax.ShapeDtypeStruct((512, 512), BF), in...]
where the time goes in v8:
time: 63.1 us; the launch traced here: 63 us
  Pallas kernels  61.1 us (97%)
  local copies, waits for them, and re-layouts  1.87 us (3%)
    pallas_call x1, Pallas kernels, body(): pl.pallas_call(kernel, out_shape=jax.ShapeDtypeStruct((512, 512), BF), in...  61.1 us
    unnamed x1, local copies, waits for them, and re-layouts  1.87 us

profile of v8, /device:TPU:1, one launch (start us, length us, event | category | flops | bytes accessed | tf_op | source)
XLA Modules:
  0.0 63.0 jit_solution(12055462320841666852)
XLA Ops:
  0.0 61.1 %shard_map.46 = bf16[512,512]{1,0:T(8,128)(2,1)} custom-call(bf16[512,2048]{1,0:T(8,128)(2,1)} %bitcast.2, bf16[512,1536]{1,0:T(8,128)(2,1)} %wgt.1, s32[4]{0:T(128)} %noff_h.1, s32[4]{0:T(128)} %foff_h.1), custom_call_target="tpu_custom_call" | custom-call | tf_op jit(solution)/shard_map/pallas_call | solution.py:474
  61.1 1.9 %copy.6 = bf16[1,512,512]{2,1,0:T(8,128)(2,1)} copy(bf16[1,512,512]{2,1,0:T(8,128)(2,1)} %bitcast.3) | data formatting | bytes 1048576

commit v9 on v8

--- a/solution.py
+++ b/solution.py
@@ -509,7 +509,7 @@
             pltpu.SemaphoreType.DMA((9,)),
         ],
         compiler_params=pltpu.CompilerParams(
-            collective_id=0, has_side_effects=True, vmem_limit_bytes=60 * 1024 * 1024),
+            collective_id=0, has_side_effects=True, vmem_limit_bytes=52 * 1024 * 1024),
     )(tokens[0], qkv_weight, near_offset, far_offset)
     return mixed[None]
 

time: 63.1 us -> 62.6 us (level)
  Pallas kernels: 61.1 us -> 60.3 us
    pallas_call x1, Pallas kernels: 61.1 us -> 60.3 us  [body(): pl.pallas_call(kernel, out_shape=jax.ShapeDtypeStruct((512, 512), BF), in...]
    unnamed x1 -> x5, local copies, waits for them, and re-layouts: 1.87 us -> 2.11 us
where the time goes in v9:
time: 62.6 us; the launch traced here: 62.4 us
  Pallas kernels  60.3 us (96%)
  local copies, waits for them, and re-layouts  2.11 us (3%)
    pallas_call x1, Pallas kernels, body(): pl.pallas_call(kernel, out_shape=jax.ShapeDtypeStruct((512, 512), BF), in...  60.3 us
    unnamed x5, local copies, waits for them, and re-layouts  2.11 us

profile of v9, /device:TPU:1, one launch (start us, length us, event | category | flops | bytes accessed | tf_op | source)
XLA Modules:
  0.0 62.4 jit_solution(6756386307004018220)
XLA Ops:
  0.0 0.0 copy-start
  0.0 0.7 %copy-done = s32[4]{0:T(128)S(1)} copy-done((s32[4]{0:T(128)S(1)}, s32[4]{0:T(128)}, u32[]{:S(2)}) %copy-start) | copy-done | bytes 40
  0.7 0.0 copy-start.1
  0.7 0.7 %copy-done.1 = s32[4]{0:T(128)S(1)} copy-done((s32[4]{0:T(128)S(1)}, s32[4]{0:T(128)}, u32[]{:S(2)}) %copy-start.1) | copy-done | bytes 40
  1.3 60.3 %shard_map.46 = bf16[512,512]{1,0:T(8,128)(2,1)S(1)} custom-call(bf16[512,2048]{1,0:T(8,128)(2,1)} %bitcast.3, bf16[512,1536]{1,0:T(8,128)(2,1)} %wgt.1, s32[4]{0:T(128)S(1)} %copy-done, s32[4]{0:T(128)S(1)} %copy-done.1), custom_call_target="tpu_custom_call" | custom-call | tf_op jit(solution)/shard_map/pallas_call | solution.py:474
  61.6 0.8 %copy.6 = bf16[1,512,512]{2,1,0:T(8,128)(2,1)} copy(bf16[1,512,512]{2,1,0:T(8,128)(2,1)S(1)} %bitcast.2) | data formatting | bytes 1048576
Async XLA Ops:
  0.0 0.7 %copy-start = (s32[4]{0:T(128)S(1)}, s32[4]{0:T(128)}, u32[]{:S(2)}) copy-start(s32[4]{0:T(128)} %noff_h.1) | copy-start | bytes 52
  0.7 0.7 %copy-start.1 = (s32[4]{0:T(128)S(1)}, s32[4]{0:T(128)}, u32[]{:S(2)}) copy-start(s32[4]{0:T(128)} %foff_h.1) | copy-start | bytes 52
